TPU v7x, 1024 devices: a whole 4x8x16 slice. The times are simulated.
1024 devices in a mesh: tm: 32 (over z, core), space: 4 (over x), node: 8 (over y).
Axes of the slice: x: 4, y: 8, z: 16, core: 2. Of those that a mesh axis runs over, the one named last changes fastest.
Arguments:
- initial: float32 [8, 64, 256], P(None, 'space'), may hold values from -6 to 6
- forcing: float32 [32, 8, 64, 256], P('tm', None, 'space'), may hold values from -6 to 6
- decay_rate: float32 [8, 64, 256], P(None, 'space'), may hold values from 0.02 to 20
- mixing: float32 [8, 8], replicated, may hold values from -2 to 2
- diffusivity: float32 [8], replicated, may hold values from 0.3 to 2
- velocity: float32 [3, 8], replicated, may hold values from -2 to 2
Outputs:
- node_values: float32 [32, 8, 8, 64, 256], P('tm', 'node', None, 'space')
All inputs are finite; a program needn't handle non-finite values.
Results may differ from a plain program's by a relative error of at most 0.0003.
Values sent between devices are 32-bit elements; how exact they have to be, the bound alone decides.
No kernel may reach another device: no remote copies, remote signals or barrier semaphores. Data moves between devices by JAX's collectives and lax.ppermute only.
A program may use at most 32 MiB of HBM per device.

v0:
```python
import jax
import jax.numpy as jnp
import numpy as np
from jax import lax
from jax.sharding import PartitionSpec as P

NZ = 16


time_step = 0.05


def carried_in(part, axis, combine, identity):
    place = lax.axis_index(axis)
    gathered = jax.tree.map(lambda a: lax.all_gather(a, axis), part)
    state = jax.tree.map(lambda a, e: jnp.zeros_like(a) + jnp.asarray(e, a.dtype), part, identity)

    def one(lap, state):
        return combine(
            state, jax.tree.map(lambda a: lax.dynamic_index_in_dim(a, lap, 0, False), gathered)
        )

    return lax.fori_loop(0, place, one, state)


def extended(value, sides, width):
    for axis, dim in sides:
        peers, length = (lax.axis_size(axis), value.shape[dim])
        up = [(i, (i + 1) % peers) for i in range(peers - 1)]
        down = [(j, i) for i, j in up]
        last = lax.slice_in_dim(value, length - width, length, axis=dim)
        initial = lax.slice_in_dim(value, 0, width, axis=dim)
        before = lax.ppermute(last, axis, up)
        after = lax.ppermute(initial, axis, down)
        value = jnp.concatenate([before, value, after], axis=dim)
    return value


def from_behind(block, axis, distance):
    devices = range(lax.axis_size(axis))
    route = [(i - distance, i) for i in devices if i - distance in devices]
    return lax.ppermute(block, axis, route)


def quadrature(node_count):
    points = [(position + 1.0) / node_count for position in range(node_count)]
    weights_table = np.zeros((node_count, node_count))
    for column in range(node_count):
        coeffs = [1.0]
        denominator = 1.0
        for other_node in range(node_count):
            if other_node != column:
                shifted = [0.0] + coeffs
                for degree in range(len(coeffs)):
                    shifted[degree] = shifted[degree] - points[other_node] * coeffs[degree]
                coeffs = shifted
                denominator = denominator * (points[column] - points[other_node])
        for row_node in range(node_count):
            running = 0.0
            for degree in range(len(coeffs)):
                running = running + coeffs[degree] * points[row_node] ** (degree + 1) / (degree + 1)
            weights_table[row_node, column] = running / denominator
    return (weights_table, np.array(points))


def rate_of(padded, decay_rate, mixing, diffusivity, velocity, force_now):
    center = padded[:, 1:-1]
    x_plus = padded[:, 2:]
    x_minus = padded[:, :-2]
    y_plus = jnp.roll(center, -NZ, axis=2)
    y_minus = jnp.roll(center, NZ, axis=2)
    depth_index = jnp.arange(center.shape[2]) % NZ
    z_plus = jnp.where(depth_index == NZ - 1, 0.0, jnp.roll(center, -1, axis=2))
    z_minus = jnp.where(depth_index == 0, 0.0, jnp.roll(center, 1, axis=2))
    laplace = x_plus + x_minus + (y_plus + y_minus) + (z_plus + z_minus) - 6.0 * center
    drift_term = (
        velocity[0][:, None, None] * (x_plus - x_minus)
        + velocity[1][:, None, None] * (y_plus - y_minus)
        + velocity[2][:, None, None] * (z_plus - z_minus)
    )
    coupled = jnp.tanh(jnp.einsum("ts,sxc->txc", mixing, center, precision=lax.Precision.HIGHEST))
    return (
        diffusivity[:, None, None] * laplace
        - 0.5 * drift_term
        - decay_rate * center
        + coupled
        + force_now
    )


def body(initial, forcing, decay_rate, mixing, diffusivity, velocity):
    node_count = lax.axis_size("node")
    node_index = lax.axis_index("node")
    weights_table, points = quadrature(node_count)
    q_table = jnp.asarray(weights_table, jnp.float32)
    time_table = jnp.asarray(points, jnp.float32)
    own_match = jnp.arange(node_count) == node_index
    own_row = jnp.sum(jnp.where(own_match[:, None], q_table, 0.0), axis=0)
    last_row = q_table[node_count - 1]
    own_time = jnp.sum(jnp.where(own_match, time_table, 0.0))
    last_time = time_table[node_count - 1]
    stiff_part = time_step * (own_time / node_count) * decay_rate
    last_stiff = time_step * (last_time / node_count) * decay_rate
    force_now = forcing[0]
    factor = 1.0 / (1.0 + time_step * decay_rate)
    offset = time_step * force_now * factor

    def compose(earlier, later):
        return (earlier[0] * later[0], later[0] * earlier[1] + later[1])

    prefix = carried_in(
        (factor, offset), "tm", compose, (jnp.ones_like(factor), jnp.zeros_like(offset))
    )
    slice_start = prefix[0] * initial + prefix[1]

    def local_rate(field_now):
        padded = extended(field_now, (("space", 1),), 1)
        return rate_of(padded, decay_rate, mixing, diffusivity, velocity, force_now)

    def weighted_sums(field_now):
        rate_now = local_rate(field_now)
        empty = jnp.zeros_like(rate_now)
        shard_piece = lax.all_gather(rate_now[None], "node", axis=0, tiled=True)
        return (
            empty + jnp.sum(own_row[:, None, None, None] * shard_piece, axis=0),
            empty + jnp.sum(last_row[:, None, None, None] * shard_piece, axis=0),
        )

    first_value = (slice_start + own_time * time_step * force_now) / (
        1.0 + own_time * time_step * decay_rate
    )
    last_first = (slice_start + last_time * time_step * force_now) / (
        1.0 + last_time * time_step * decay_rate
    )
    own_sum, end_sum = weighted_sums(first_value)
    second_value = (slice_start + time_step * own_sum + stiff_part * first_value) / (
        1.0 + stiff_part
    )
    end_value = (slice_start + time_step * end_sum + last_stiff * last_first) / (1.0 + last_stiff)
    handed = from_behind(end_value, "tm", 1)
    second_start = jnp.where(lax.axis_index("tm") == 0, initial, handed)
    own_next, unused_end = weighted_sums(second_value)
    final_value = (second_start + time_step * own_next + stiff_part * second_value) / (
        1.0 + stiff_part
    )
    return final_value[None, None]


def solution(mesh):
    placed = (
        P(None, "space", None),
        P("tm", None, "space", None),
        P(None, "space", None),
        P(),
        P(),
        P(),
    )
    return jax.shard_map(
        body,
        mesh=mesh,
        in_specs=placed,
        out_specs=P("tm", "node", None, "space", None),
        check_vma=False,
    )
```

profile of v0, /device:TPU:8, one launch (start us, length us, event | category | flops | bytes accessed | tf_op | source)
XLA Modules:
  0.0 321.9 jit_solution(6199390623273553001)
XLA Ops:
  6.5 0.0 copy-start
  6.5 0.0 all-gather.9.cloned.1.call-start
  6.6 1.9 fusion.14
  8.5 0.0 all-gather.9.cloned.1.call-update
  8.5 0.0 all-gather.11.cloned.1.call-start
  8.6 0.7 all-gather.11.cloned.1.call-update
  9.3 0.0 all-gather.13.cloned.1.call-start
  9.3 1.3 select_reduce_fusion.1
  11.2 0.8 slice_bitcast_fusion.2
  12.0 83.8 %all-gather.9.cloned.1.call-done = f32[256,16,256]{2,0,1:T(8,128)} async-done(((f32[8,16,256]{2,0,1:T(8,128)}), f32[256,16,256]{2,0,1:T(8,128)}) %all-gather.9.cloned.1.call-update) | async-done | bytes 4194320 | tf_op jit(solution)/shard_map/all_gather | solution.py:15
  95.7 76.8 %all-gather.11.cloned.1.call-done = f32[256,16,256]{2,0,1:T(8,128)} async-done(((f32[8,16,256]{2,0,1:T(8,128)}), f32[256,16,256]{2,0,1:T(8,128)}) %all-gather.11.cloned.1.call-update) | async-done | bytes 4194320 | tf_op jit(solution)/shard_map/all_gather | solution.py:15
  172.6 0.0 copy-start.6
  172.6 0.0 copy-start.4
  172.6 0.0 copy-start.5
  172.7 0.0 copy-done.2
  172.7 0.4 fusion.12
  173.1 0.1 fusion.23
  173.2 0.1 fusion.25
  173.3 0.1 fusion.24
  173.4 1.3 collective-permute-start
  174.7 4.5 %collective-permute-start.1 = (f32[8,1,256]{2,0,1:T(8,128)S(1)}, f32[8,1,256]{2,0,1:T(8,128)S(1)}, u32[]{:S(2)}, u32[]{:S(2)}) collective-permute-start(f32[8,1,256]{2,0,1:T(8,128)S(1)} %get-tuple-element.85), channel_id=1, source_target_pairs={{0,8},{8,16},{16,24},{1,9},{9,17},{17,25},{2,10},{10,18},{18,26},{... | collective-permute-start | bytes 24584 | tf_op jit(solution)/shard_map/ppermute | solution.py:33
  179.2 0.1 fusion.26
  179.3 0.0 collective-permute-done
  179.3 1.3 collective-permute-done.1
  180.6 0.0 copy-done.6
  180.6 1.0 fusion.6
  181.6 0.0 all-gather.13.cloned.1.call-update
  181.7 0.0 all-gather.15.cloned.1.call-start
  182.3 0.1 select_reduce_fusion
  182.4 74.1 %all-gather.13.cloned.1.call-done = f32[64,16,256]{2,0,1:T(8,128)} async-done(((f32[8,16,256]{2,0,1:T(8,128)}), f32[64,16,256]{2,0,1:T(8,128)}) %all-gather.13.cloned.1.call-update) | async-done | bytes 1048592 | tf_op jit(solution)/shard_map/all_gather | solution.py:123
  256.5 1.5 fusion.9
  257.9 0.2 add_divide_fusion.1
  258.2 0.1 fusion.18
  258.3 0.1 fusion.20
  258.4 0.1 fusion.19
  258.5 1.3 collective-permute-start.3
  259.8 4.5 %collective-permute-start.4 = (f32[8,1,256]{2,0,1:T(8,128)S(1)}, f32[8,1,256]{2,0,1:T(8,128)S(1)}, u32[]{:S(2)}, u32[]{:S(2)}) collective-permute-start(f32[8,1,256]{2,0,1:T(8,128)S(1)} %get-tuple-element.75), channel_id=1, source_target_pairs={{0,8},{8,16},{16,24},{1,9},{9,17},{17,25},{2,10},{10,18},{18,26},{... | collective-permute-start | bytes 24584 | tf_op jit(solution)/shard_map/ppermute | solution.py:33
  264.3 0.1 fusion.21
  264.4 0.0 collective-permute-done.3
  264.4 1.3 collective-permute-done.4
  265.7 1.0 fusion.7
  266.7 0.0 all-gather.15.cloned.1.call-update
  266.7 1.3 collective-permute-start.2
  268.0 45.0 %all-gather.15.cloned.1.call-done = f32[64,16,256]{2,0,1:T(8,128)} async-done(((f32[8,16,256]{2,0,1:T(8,128)}), f32[64,16,256]{2,0,1:T(8,128)}) %all-gather.15.cloned.1.call-update) | async-done | bytes 1048592 | tf_op jit(solution)/shard_map/all_gather | solution.py:123
  313.1 1.4 fusion.8
  314.4 0.0 collective-permute-done.2
  314.5 0.2 divide_bitcast_fusion
  314.7 0.7 copy.40
  (15 shorter events, 0.1 us)
Async XLA Ops:
  6.5 174.1 %copy-start = (f32[8,8]{1,0:T(8,128)S(1)}, f32[8,8]{1,0:T(8,128)}, u32[]{:S(2)}) copy-start(f32[8,8]{1,0:T(8,128)} %param.13) | copy-start | bytes 772
  6.5 166.1 %copy-start.2 = (f32[1,8,16,256]{3,2,1,0:T(8,128)S(1)}, f32[1,8,16,256]{3,2,1,0:T(8,128)}, u32[]{:S(2)}) copy-start(f32[1,8,16,256]{3,2,1,0:T(8,128)} %param.11) | copy-start | bytes 393220
  6.5 166.1 %copy-start.1 = (f32[8,16,256]{2,1,0:T(8,128)S(1)}, f32[8,16,256]{2,1,0:T(8,128)}, u32[]{:S(2)}) copy-start(f32[8,16,256]{2,1,0:T(8,128)} %param.12) | copy-start | bytes 393220
  6.5 166.1 %copy-start.3 = (f32[8,16,256]{2,1,0:T(8,128)S(1)}, f32[8,16,256]{2,1,0:T(8,128)}, u32[]{:S(2)}) copy-start(f32[8,16,256]{2,1,0:T(8,128)} %param.10) | copy-start | bytes 393220
  6.5 89.2 %all-gather.9.cloned.1.call-start = ((), (), s32[]{:S(2)}) async-start(), calls=%async_computation | async-start | bytes 4325376 | tf_op jit(solution)/shard_map/all_gather | solution.py:15
  8.5 164.0 %all-gather.11.cloned.1.call-start = ((), (), s32[]{:S(2)}) async-start(), calls=%async_computation.1 | async-start | bytes 4325376 | tf_op jit(solution)/shard_map/all_gather | solution.py:15
  9.3 247.2 %all-gather.13.cloned.1.call-start = ((), (), s32[]{:S(2)}) async-start(), calls=%async_computation.2 | async-start | bytes 1179648 | tf_op jit(solution)/shard_map/all_gather | solution.py:123
  172.6 8.0 %copy-start.6 = (f32[8]{0:T(128)S(1)}, f32[8]{0:T(128)}, u32[]{:S(2)}) copy-start(f32[8]{0:T(128)} %param.14) | copy-start | bytes 100
  172.6 9.7 %copy-start.4 = (f32[8,8]{1,0:T(8,128)S(1)}, f32[8,8]{1,0:T(8,128)}, u32[]{:S(2)}) copy-start(f32[8,8]{1,0:T(8,128)} %constant.67.clone) | copy-start | bytes 772
  172.6 83.8 %copy-start.5 = (f32[8]{0:T(128)S(1)}, f32[8]{0:T(128)}, u32[]{:S(2)}) copy-start(f32[8]{0:T(128)} %constant.71) | copy-start | bytes 100
  173.4 5.9 %collective-permute-start = (f32[8,1,256]{2,0,1:T(8,128)S(1)}, f32[8,1,256]{2,0,1:T(8,128)S(1)}, u32[]{:S(2)}, u32[]{:S(2)}) collective-permute-start(f32[8,1,256]{2,0,1:T(8,128)S(1)} %get-tuple-element.86), channel_id=1, source_target_pairs={{8,0},{16,8},{24,16},{9,1},{17,9},{25,17},{10,2},{18,10},{26,18},{... | collective-permute-start | bytes 24584 | tf_op jit(solution)/shard_map/ppermute | solution.py:34
  174.7 5.9 %collective-permute-start.1 = (f32[8,1,256]{2,0,1:T(8,128)S(1)}, f32[8,1,256]{2,0,1:T(8,128)S(1)}, u32[]{:S(2)}, u32[]{:S(2)}) collective-permute-start(f32[8,1,256]{2,0,1:T(8,128)S(1)} %get-tuple-element.85), channel_id=1, source_target_pairs={{0,8},{8,16},{16,24},{1,9},{9,17},{17,25},{2,10},{10,18},{18,26},{... | collective-permute-start | bytes 24584 | tf_op jit(solution)/shard_map/ppermute | solution.py:33
  181.7 131.4 %all-gather.15.cloned.1.call-start = ((), (), s32[]{:S(2)}) async-start(), calls=%async_computation.3 | async-start | bytes 1179648 | tf_op jit(solution)/shard_map/all_gather | solution.py:123
  258.5 5.9 %collective-permute-start.3 = (f32[8,1,256]{2,0,1:T(8,128)S(1)}, f32[8,1,256]{2,0,1:T(8,128)S(1)}, u32[]{:S(2)}, u32[]{:S(2)}) collective-permute-start(f32[8,1,256]{2,0,1:T(8,128)S(1)} %get-tuple-element.76), channel_id=1, source_target_pairs={{8,0},{16,8},{24,16},{9,1},{17,9},{25,17},{10,2},{18,10},{26,18},{... | collective-permute-start | bytes 24584 | tf_op jit(solution)/shard_map/ppermute | solution.py:34
  259.8 5.9 %collective-permute-start.4 = (f32[8,1,256]{2,0,1:T(8,128)S(1)}, f32[8,1,256]{2,0,1:T(8,128)S(1)}, u32[]{:S(2)}, u32[]{:S(2)}) collective-permute-start(f32[8,1,256]{2,0,1:T(8,128)S(1)} %get-tuple-element.75), channel_id=1, source_target_pairs={{0,8},{8,16},{16,24},{1,9},{9,17},{17,25},{2,10},{10,18},{18,26},{... | collective-permute-start | bytes 24584 | tf_op jit(solution)/shard_map/ppermute | solution.py:33
  266.7 47.7 %collective-permute-start.2 = (f32[8,16,256]{2,0,1:T(8,128)S(1)}, f32[8,16,256]{2,0,1:T(8,128)S(1)}, u32[]{:S(2)}, u32[]{:S(2)}) collective-permute-start(f32[8,16,256]{2,0,1:T(8,128)S(1)} %get-tuple-element.73), channel_id=1, source_target_pairs={{0,32},{32,64},{64,96},{96,128},{128,160},{160,192},{192,224},{224... | collective-permute-start | bytes 393224 | tf_op jit(solution)/shard_map/ppermute | solution.py:42
Sparse Core Ops, SparseCore 0:
  10.1 85.5 all-gather.8
  98.5 74.0 all-gather.10
  181.8 74.6 all-gather.12
  266.9 46.1 all-gather.14
where the time goes:
time: 323 us; the launch traced here: 322 us
  waiting for transfers between devices  283 us (88%)
  between operations  14.5 us (4%)
  starting transfers between devices  13.1 us (4%)
  other arithmetic  6.91 us (2%)
    all_gather x2, waiting for transfers between devices, carried_in(): gathered = jax.tree.map(lambda a: lax.all_gather(a, axis), part)  161 us
    all_gather x2, waiting for transfers between devices, weighted_sums(): shard_piece = lax.all_gather(rate_now[None], 'node', axis=0, tiled=True)  119 us
    ppermute x2, starting transfers between devices, extended(): before = lax.ppermute(last, axis, up)  9.09 us
  transfers between devices with their start and end apart: 9, of which 6 were waited for; matrix products, arithmetic and copies ran while one was open for 1% of the time, Pallas kernels for 0%

commit v1 on v0

v1 whole, which is shorter than its diff:
```python
import jax
import jax.numpy as jnp
import numpy as np
from jax import lax
from jax.sharding import PartitionSpec as P

NZ = 16
TEAM = 4
time_step = 0.05


def quadrature(node_count):
    points = [(position + 1.0) / node_count for position in range(node_count)]
    weights_table = np.zeros((node_count, node_count))
    for column in range(node_count):
        coeffs = [1.0]
        denominator = 1.0
        for other_node in range(node_count):
            if other_node != column:
                shifted = [0.0] + coeffs
                for degree in range(len(coeffs)):
                    shifted[degree] = shifted[degree] - points[other_node] * coeffs[degree]
                coeffs = shifted
                denominator = denominator * (points[column] - points[other_node])
        for row_node in range(node_count):
            running = 0.0
            for degree in range(len(coeffs)):
                running = running + coeffs[degree] * points[row_node] ** (degree + 1) / (degree + 1)
            weights_table[row_node, column] = running / denominator
    return (weights_table, np.array(points))


def rates(v, decay_rate, mixing, diffusivity, velocity, force):
    center = v[:, :, 1:-1]
    x_plus = v[:, :, 2:]
    x_minus = v[:, :, :-2]
    y_plus = jnp.roll(center, -NZ, axis=3)
    y_minus = jnp.roll(center, NZ, axis=3)
    depth = jnp.arange(center.shape[3]) % NZ
    z_plus = jnp.where(depth == NZ - 1, 0.0, jnp.roll(center, -1, axis=3))
    z_minus = jnp.where(depth == 0, 0.0, jnp.roll(center, 1, axis=3))
    laplace = x_plus + x_minus + (y_plus + y_minus) + (z_plus + z_minus) - 6.0 * center
    drift = (
        velocity[0][:, None, None] * (x_plus - x_minus)
        + velocity[1][:, None, None] * (y_plus - y_minus)
        + velocity[2][:, None, None] * (z_plus - z_minus)
    )
    species = mixing.shape[0]
    coupled = sum(mixing[:, t][:, None, None] * center[:, t][:, None] for t in range(species))
    return (
        diffusivity[:, None, None] * laplace
        - 0.5 * drift
        - decay_rate * center
        + jnp.tanh(coupled)
        + force
    )


def slice_starts(initial, force, decay_rate):
    slices = lax.axis_size("tm")
    place = lax.axis_index("tm")
    member = place % TEAM
    team = place // TEAM
    teams = slices // TEAM
    groups = [[TEAM * g + i for i in range(TEAM)] for g in range(teams)]
    factor = 1.0 / (1.0 + time_step * decay_rate)
    handover = lax.ppermute(force, "tm", [(TEAM * g - 1, TEAM * g) for g in range(1, teams)])
    gathered = lax.all_gather(force, "tm", axis_index_groups=groups)
    share = force.shape[0] // TEAM

    def own(array, axis):
        return lax.dynamic_slice_in_dim(array, member * share, share, axis)

    own_factor = own(factor, 0)
    own_gathered = own(gathered, 1)
    total = jnp.zeros_like(own_factor)
    for k in range(TEAM):
        total = own_factor * (total + time_step * own_gathered[k])
    factor2 = own_factor * own_factor
    factor4 = factor2 * factor2
    arrived = [
        lax.ppermute(total, "tm", [(p, p + TEAM * d) for p in range(slices - TEAM * d)])
        for d in range(1, teams)
    ]
    own_initial = own(initial, 0)
    state = jnp.zeros_like(own_factor)
    for d in range(teams - 1, 0, -1):
        state = jnp.where(team == d, own_initial, state)
        state = factor4 * state + arrived[d - 1]
    state = jnp.where(team == 0, own_initial, state)
    base = lax.all_gather(state, "tm", axis=0, tiled=True, axis_index_groups=groups)

    start = base
    before = base * (1.0 + time_step * decay_rate) - time_step * handover
    force_before = handover
    for k in range(TEAM - 1):
        passed = member > k
        before = jnp.where(passed, start, before)
        force_before = jnp.where(passed, gathered[k], force_before)
        start = jnp.where(passed, factor * (start + time_step * gathered[k]), start)
    return start, before, force_before


def body(initial, forcing, decay_rate, mixing, diffusivity, velocity):
    node_count = lax.axis_size("node")
    node_index = lax.axis_index("node")
    weights_table, points = quadrature(node_count)
    q_table = jnp.asarray(weights_table, jnp.float32)
    times = jnp.asarray(points, jnp.float32)[:, None, None, None]
    own_row = lax.dynamic_index_in_dim(q_table, node_index, 0, False)
    force = forcing[0]
    start, before, force_before = slice_starts(initial, force, decay_rate)

    tiles = lax.axis_size("space")
    tile = lax.axis_index("space")
    fields = jnp.stack([start, before, force, force_before, decay_rate])
    up = [(i, i + 1) for i in range(tiles - 1)]
    down = [(j, i) for i, j in up]
    below = lax.ppermute(fields[:, :, -2:], "space", up)
    above = lax.ppermute(fields[:, :, :2], "space", down)
    fields = jnp.concatenate([below, fields, above], axis=2)
    start_w, before_w, force_w, force_before_w, decay_w = [fields[k] for k in range(5)]

    def first_sweep(start_w, force_w, decay_w, rows):
        v0 = (start_w[None] + times * time_step * force_w[None]) / (
            1.0 + times * time_step * decay_w[None]
        )
        inner = decay_w[:, 1:-1]
        rate = rates(v0, inner, mixing, diffusivity, velocity, force_w[:, 1:-1])
        out = []
        for m in rows:
            summed = sum(float(np.float32(weights_table[m, j])) * rate[j] for j in range(node_count))
            stiff = float(np.float32(time_step * points[m] / node_count)) * inner
            out.append((start_w[:, 1:-1] + time_step * summed + stiff * v0[m][:, 1:-1]) / (1.0 + stiff))
        return jnp.stack(out)

    v1 = first_sweep(start_w, force_w, decay_w, range(node_count))
    planes = v1.shape[2]
    row = jnp.arange(planes)[:, None]
    outside = ((tile == 0) & (row == 0)) | ((tile == tiles - 1) & (row == planes - 1))
    v1 = jnp.where(outside, 0.0, v1)
    inner = slice(1, -1)
    handed = first_sweep(
        before_w[:, inner], force_before_w[:, inner], decay_w[:, inner], [node_count - 1]
    )[0]
    second_start = jnp.where(
        lax.axis_index("tm") == 0, initial, handed
    )
    rate = rates(v1, decay_rate, mixing, diffusivity, velocity, force)
    summed = jnp.sum(own_row[:, None, None, None] * rate, axis=0)
    own_v1 = lax.dynamic_index_in_dim(v1, node_index, 0, False)[:, inner]
    own_time = (node_index.astype(jnp.float32) + 1.0) / node_count
    stiff = time_step * (own_time / node_count) * decay_rate
    final = (second_start + time_step * summed + stiff * own_v1) / (1.0 + stiff)
    return final[None, None]


def solution(mesh):
    placed = (
        P(None, "space", None),
        P("tm", None, "space", None),
        P(None, "space", None),
        P(),
        P(),
        P(),
    )
    return jax.shard_map(
        body,
        mesh=mesh,
        in_specs=placed,
        out_specs=P("tm", "node", None, "space", None),
        check_vma=False,
    )
```

time: 323 us -> 86 us (0.27)
  the two profiles are of different devices: /device:TPU:8 before, /device:TPU:50 now
where the time goes in v1:
time: 86 us; the launch traced here: 85.5 us
  starting transfers between devices  41.2 us (48%)
  other arithmetic  15.3 us (18%)
  blocking collectives  13.8 us (16%)
  local copies, waits for them, and re-layouts  11.6 us (13%)
  waiting for transfers between devices  3.06 us (4%)
    ppermute x7, starting transfers between devices, slice_starts(): lax.ppermute(total, 'tm', [(p, p + TEAM * d) for p in range(slices - TEAM...  34.7 us
    all_gather x1, blocking collectives, slice_starts(): gathered = lax.all_gather(force, 'tm', axis_index_groups=groups)  8.38 us
    add x2, other arithmetic, rates(): diffusivity[:, None, None] * laplace - 0.5 * drift - decay_rate * center  5.64 us
    all_gather x1, blocking collectives, slice_starts(): lax.all_gather(state, 'tm', axis=0, tiled=True, axis_index_groups=groups)  5.42 us
    ppermute x1, starting transfers between devices, body(): below = lax.ppermute(fields[:, :, -2:], 'space', up)  3.4 us
    ppermute x1, waiting for transfers between devices, body(): above = lax.ppermute(fields[:, :, :2], 'space', down)  2.68 us
    reduce_sum x1, other arithmetic, body(): summed = jnp.sum(own_row[:, None, None, None] * rate, axis=0)  2.59 us
    unnamed x10, other arithmetic  2.55 us
  transfers between devices with their start and end apart: 10, of which 2 were waited for; matrix products, arithmetic and copies ran while one was open for 5% of the time, Pallas kernels for 0%

profile of v1, /device:TPU:50, one launch (start us, length us, event | category | flops | bytes accessed | tf_op | source)
XLA Modules:
  0.0 85.5 jit_solution(10268896840131810342)
XLA Ops:
  0.0 8.4 %all_gather.6 = f32[4,8,16,256]{3,2,1,0:T(8,128)S(1)} all-gather(f32[1,8,16,256]{3,2,1,0:T(8,128)} %param.9), channel_id=1, replica_groups={{0,32,64,96},{128,160,192,224},{256,288,320,352},{384,416,448,480},{512..., dimensions={0}, use_global_device_ids=true | all-gather | bytes 655360 | tf_op jit(solution)/shard_map/all_gather | solution.py:68
  8.4 0.9 %fusion.49 = f32[8,16,256]{2,1,0:T(8,128)S(1)} fusion(f32[8,16,256]{2,1,0:T(8,128)} %param.10), kind=kLoop, calls=%fused_computation.143 | loop fusion | flops 98304 | bytes 262144 | tf_op jit(solution)/shard_map/div | solution.py:66
  9.4 17.3 %collective-permute-start = (f32[2,16,256]{2,1,0:T(8,128)S(1)}, f32[2,16,256]{2,1,0:T(8,128)S(1)}, u32[]{:S(2)}, u32[]{:S(2)}) collective-permute-start(f32[2,16,256]{2,1,0:T(8,128)S(1)} %fusion.52), channel_id=1, source_target_pairs={{0,896},{32,928},{64,960},{96,992},{1,897},{33,929},{65,961},{97,9... | collective-permute-start | bytes 98312 | tf_op jit(solution)/shard_map/ppermute | solution.py:82
  26.7 1.3 %collective-permute-start.1 = (f32[2,16,256]{2,1,0:T(8,128)S(1)}, f32[2,16,256]{2,1,0:T(8,128)S(1)}, u32[]{:S(2)}, u32[]{:S(2)}) collective-permute-start(f32[2,16,256]{2,1,0:T(8,128)S(1)} %fusion.52), channel_id=1, source_target_pairs={{0,768},{32,800},{64,832},{96,864},{128,896},{160,928},{192,960},{... | collective-permute-start | bytes 98312 | tf_op jit(solution)/shard_map/ppermute | solution.py:82
  28.0 1.3 %collective-permute-start.2 = (f32[2,16,256]{2,1,0:T(8,128)S(1)}, f32[2,16,256]{2,1,0:T(8,128)S(1)}, u32[]{:S(2)}, u32[]{:S(2)}) collective-permute-start(f32[2,16,256]{2,1,0:T(8,128)S(1)} %fusion.52), channel_id=1, source_target_pairs={{0,640},{32,672},{64,704},{96,736},{128,768},{160,800},{192,832},{... | collective-permute-start | bytes 98312 | tf_op jit(solution)/shard_map/ppermute | solution.py:82
  29.3 1.3 %collective-permute-start.3 = (f32[2,16,256]{2,1,0:T(8,128)S(1)}, f32[2,16,256]{2,1,0:T(8,128)S(1)}, u32[]{:S(2)}, u32[]{:S(2)}) collective-permute-start(f32[2,16,256]{2,1,0:T(8,128)S(1)} %fusion.52), channel_id=1, source_target_pairs={{0,512},{32,544},{64,576},{96,608},{128,640},{160,672},{192,704},{... | collective-permute-start | bytes 98312 | tf_op jit(solution)/shard_map/ppermute | solution.py:82
  30.6 9.1 %collective-permute-start.4 = (f32[2,16,256]{2,1,0:T(8,128)S(1)}, f32[2,16,256]{2,1,0:T(8,128)S(1)}, u32[]{:S(2)}, u32[]{:S(2)}) collective-permute-start(f32[2,16,256]{2,1,0:T(8,128)S(1)} %fusion.52), channel_id=1, source_target_pairs={{0,384},{32,416},{64,448},{96,480},{128,512},{160,544},{192,576},{... | collective-permute-start | bytes 98312 | tf_op jit(solution)/shard_map/ppermute | solution.py:82
  39.7 1.3 %slice_reduce_fusion.7 = (f32[8]{0:T(128)S(1)}, f32[8]{0:T(128)S(1)}, f32[8]{0:T(128)S(1)}, f32[8]{0:T(128)S(1)}, f32[8]{0:T(128)S(1)}, /*index=5*/f32[8]{0:T(128)S(1)}, f32[8]{0:T(128)S(1)}, f32[8]{0:T(128)S(1)}) fusion(f32[8,8]{1,0:T(8,128)} %param.11), kind=kLoop, calls=%fused_computation.168 | loop fusion | bytes 512 | tf_op jit(solution)/shard_map/slice | solution.py:49
  40.9 0.8 slice_bitcast_fusion.43
  41.8 1.3 %collective-permute-start.5 = (f32[2,16,256]{2,1,0:T(8,128)S(1)}, f32[2,16,256]{2,1,0:T(8,128)S(1)}, u32[]{:S(2)}, u32[]{:S(2)}) collective-permute-start(f32[2,16,256]{2,1,0:T(8,128)S(1)} %fusion.52), channel_id=1, source_target_pairs={{0,256},{32,288},{64,320},{96,352},{128,384},{160,416},{192,448},{... | collective-permute-start | bytes 98312 | tf_op jit(solution)/shard_map/ppermute | solution.py:82
  43.1 3.1 %collective-permute-start.6 = (f32[2,16,256]{2,1,0:T(8,128)S(1)}, f32[2,16,256]{2,1,0:T(8,128)S(1)}, u32[]{:S(2)}, u32[]{:S(2)}) collective-permute-start(f32[2,16,256]{2,1,0:T(8,128)S(1)} %fusion.52), channel_id=1, source_target_pairs={{0,128},{32,160},{64,192},{96,224},{128,256},{160,288},{192,320},{... | collective-permute-start | bytes 98312 | tf_op jit(solution)/shard_map/ppermute | solution.py:82
  46.2 0.5 and_or_fusion
  46.7 0.7 collective-permute-start.7
  47.4 0.4 collective-permute-done.6
  47.7 0.8 add_select_fusion
  48.6 5.4 %all_gather.7 = f32[8,16,256]{2,1,0:T(8,128)S(1)} all-gather(f32[2,16,256]{2,1,0:T(8,128)S(1)} %add_select_fusion), channel_id=1, replica_groups={{0,32,64,96},{128,160,192,224},{256,288,320,352},{384,416,448,480},{512..., dimensions={0}, use_global_device_ids=true | all-gather | bytes 163840 | tf_op jit(solution)/shard_map/all_gather | solution.py:91
  54.3 3.4 %collective-permute-start.8 = (f32[5,8,2,256]{3,2,1,0:T(2,128)S(1)}, f32[5,8,2,256]{3,2,1,0:T(2,128)S(1)}, u32[]{:S(2)}, u32[]{:S(2)}) collective-permute-start(f32[5,8,2,256]{3,2,1,0:T(2,128)S(1)} %get-tuple-element.74), channel_id=1, source_target_pairs={{0,8},{8,16},{16,24},{1,9},{9,17},{17,25},{2,10},{10,18},{18,26},{... | collective-permute-start | bytes 245768 | tf_op jit(solution)/shard_map/ppermute | solution.py:119
  57.7 2.4 %collective-permute-start.9 = (f32[5,8,2,256]{3,2,1,0:T(2,128)S(1)}, f32[5,8,2,256]{3,2,1,0:T(2,128)S(1)}, u32[]{:S(2)}, u32[]{:S(2)}) collective-permute-start(f32[5,8,2,256]{3,2,1,0:T(2,128)S(1)} %get-tuple-element.75), channel_id=1, source_target_pairs={{8,0},{16,8},{24,16},{9,1},{17,9},{25,17},{10,2},{18,10},{26,18},{... | collective-permute-start | bytes 245768 | tf_op jit(solution)/shard_map/ppermute | solution.py:120
  60.2 1.2 %fusion.61 = f32[8]{0:T(128)} fusion(f32[8,8]{1,0:T(8,128)} %constant.246.clone, s32[]{:T(128)S(6)} %select_n.202), kind=kLoop, calls=%fused_computation.172 | loop fusion | bytes 68 | tf_op jit(solution)/shard_map/mul | solution.py:150
  61.4 2.7 %collective-permute-done.9 = f32[5,8,2,256]{3,2,1,0:T(2,128)S(1)} collective-permute-done((f32[5,8,2,256]{3,2,1,0:T(2,128)S(1)}, f32[5,8,2,256]{3,2,1,0:T(2,128)S(1)}, u32[]{:S(2)}, u32[]{:S(2)}) %collective-permute-start.9) | collective-permute-done | bytes 81952 | tf_op jit(solution)/shard_map/ppermute | solution.py:120
  64.3 0.4 add_divide_fusion
  64.7 0.6 fusion.70
  65.3 0.6 fusion.72
  66.1 0.3 fusion.71
  66.4 0.3 fusion.73
  66.7 1.0 %slice_bitcast_fusion = (f32[8,20,256]{2,1,0:T(8,128)S(1)}, f32[8,20,256]{2,1,0:T(8,128)S(1)}, f32[8,20,256]{2,1,0:T(8,128)}, f32[8,20,256]{2,1,0:T(8,128)}, f32...) fusion(f32[8,8,20,256]{3,2,1,0:T(8,128)S(1)} %add_divide_fusion), kind=kLoop, calls=%fused_computation.24 | loop fusion | bytes 2621440 | tf_op jit(solution)/shard_map/squeeze | solution.py:134
  67.7 3.2 %add_add_fusion = f32[8,8,18,256]{3,2,1,0:T(8,128)S(1)} fusion(f32[8,8,20,256]{3,2,1,0:T(8,128)S(1)} %add_divide_fusion, f32[8,8,18,255]{3,2,1,0:T(8,128)S(1)} %get-tuple-element.66, f32[8,8,18,1]{3,2,1,0:T(8,128)S(1)} %get-tuple-element.68, f32[8,8,18,1]{3,2,1,0:T(8,128)S(1)} %get-tuple-element.67, f32[8,8,18,255]{3,2,1,0:T(8,128)S(1)} %get-tuple-element.65, ...), kind=kLoop, calls=%fused_computation.4 | loop fusion | flops 12681216 | bytes 10912640 | tf_op jit(solution)/shard_map/add | solution.py:51
  70.9 1.2 %fusion.31 = f32[8,8,18,256]{3,2,1,0:T(8,128)S(1)} fusion(f32[8,20,256]{2,1,0:T(8,128)} %get-tuple-element.51, f32[8,8,18,256]{3,2,1,0:T(8,128)S(1)} %add_add_fusion, f32[8,20,256]{2,1,0:T(8,128)S(1)} %get-tuple-element.71, f32[8,20,256]{2,1,0:T(8,128)S(1)} %get-tuple-element.72), kind=kLoop, calls=%fused_computation.65 | loop fusion | flops 811007 | bytes 1818624
  72.1 0.2 fusion.27
  72.3 0.7 copy-done.4
  73.5 0.7 copy-done.2
  74.4 0.2 fusion.11
  74.6 0.2 fusion.7
  75.0 0.4 copy-done.10
  75.4 0.2 broadcast_select_fusion
  75.6 0.4 fusion.62
  76.1 0.5 fusion.64
  76.7 0.2 fusion.63
  76.9 0.2 fusion.65
  77.2 0.4 add_divide_fusion.1
  77.6 0.4 fusion.66
  78.1 0.5 fusion.68
  78.7 0.2 fusion.67
  78.9 0.2 fusion.69
  79.2 0.3 copy-done.9
  79.5 2.6 %multiply_reduce_fusion = f32[8,16,256]{2,1,0:T(8,128)S(1)} fusion(f32[8,8,18,256]{3,2,1,0:T(8,128)S(1)} %broadcast_select_fusion, f32[8,8,16,255]{3,2,1,0:T(8,128)S(1)} %get-tuple-element.26, f32[8,8,16,1]{3,2,1,0:T(8,128)S(1)} %get-tuple-element.28, f32[8,8,16,1]{3,2,1,0:T(8,128)S(1)} %get-tuple-element.27, f32[8,8,16,255]{3,2,1,0:T(8,128)S(1)} %get-tuple-element.25, ...), kind=kLoop, calls=%fused_computation.15 | loop fusion | flops 11763712 | bytes 8782752 | tf_op jit(solution)/shard_map/reduce_sum | solution.py:150
  82.1 2.4 %add_add_fusion.1 = f32[8,8,16,256]{3,2,1,0:T(8,128)S(1)} fusion(f32[8,8,18,256]{3,2,1,0:T(8,128)S(1)} %add_divide_fusion.1, f32[8,8,16,255]{3,2,1,0:T(8,128)S(1)} %get-tuple-element.42, f32[8,8,16,1]{3,2,1,0:T(8,128)S(1)} %get-tuple-element.44, f32[8,8,16,1]{3,2,1,0:T(8,128)S(1)} %get-tuple-element.43, f32[8,8,16,255]{3,2,1,0:T(8,128)S(1)} %get-tuple-element.41, ...), kind=kLoop, calls=%fused_computation.16 | loop fusion | flops 11272192 | bytes 9700224 | tf_op jit(solution)/shard_map/add | solution.py:51
  84.6 0.9 %fusion.34 = f32[1,1,8,16,256]{4,3,2,1,0:T(8,128)} fusion(f32[8,18,256]{2,1,0:T(8,128)S(1)} %dynamic-slice_bitcast_fusion, f32[8,16,256]{2,1,0:T(8,128)S(1)} %copy-done.6, f32[8,18,256]{2,1,0:T(8,128)S(1)} %slice_bitcast_fusion.18, f32[8,8,16,256]{3,2,1,0:T(8,128)S(1)} %add_add_fusion.1, f32[8,20,256]{2,1,0:T(8,128)S(1)} %get-tuple-element.69, ...), kind=kLoop, calls=%fused_computation.93 | loop fusion | flops 983040 | bytes 2097157 | tf_op jit(solution)/shard_map/broadcast_in_dim | solution.py:155
  (51 shorter events, 2.1 us)
Async XLA Ops:
  0.0 54.0 %copy-start = (f32[8,16,256]{2,1,0:T(8,128)S(1)}, f32[8,16,256]{2,1,0:T(8,128)}, u32[]{:S(2)}) copy-start(f32[8,16,256]{2,1,0:T(8,128)} %param.10) | copy-start | bytes 393220
  0.0 54.2 %copy-start.1 = (f32[1,8,16,256]{3,2,1,0:T(8,128)S(1)}, f32[1,8,16,256]{3,2,1,0:T(8,128)}, u32[]{:S(2)}) copy-start(f32[1,8,16,256]{3,2,1,0:T(8,128)} %param.9) | copy-start | bytes 393220
  9.4 32.4 %collective-permute-start = (f32[2,16,256]{2,1,0:T(8,128)S(1)}, f32[2,16,256]{2,1,0:T(8,128)S(1)}, u32[]{:S(2)}, u32[]{:S(2)}) collective-permute-start(f32[2,16,256]{2,1,0:T(8,128)S(1)} %fusion.52), channel_id=1, source_target_pairs={{0,896},{32,928},{64,960},{96,992},{1,897},{33,929},{65,961},{97,9... | collective-permute-start | bytes 98312 | tf_op jit(solution)/shard_map/ppermute | solution.py:82
  26.7 16.4 %collective-permute-start.1 = (f32[2,16,256]{2,1,0:T(8,128)S(1)}, f32[2,16,256]{2,1,0:T(8,128)S(1)}, u32[]{:S(2)}, u32[]{:S(2)}) collective-permute-start(f32[2,16,256]{2,1,0:T(8,128)S(1)} %fusion.52), channel_id=1, source_target_pairs={{0,768},{32,800},{64,832},{96,864},{128,896},{160,928},{192,960},{... | collective-permute-start | bytes 98312 | tf_op jit(solution)/shard_map/ppermute | solution.py:82
  28.0 18.7 %collective-permute-start.2 = (f32[2,16,256]{2,1,0:T(8,128)S(1)}, f32[2,16,256]{2,1,0:T(8,128)S(1)}, u32[]{:S(2)}, u32[]{:S(2)}) collective-permute-start(f32[2,16,256]{2,1,0:T(8,128)S(1)} %fusion.52), channel_id=1, source_target_pairs={{0,640},{32,672},{64,704},{96,736},{128,768},{160,800},{192,832},{... | collective-permute-start | bytes 98312 | tf_op jit(solution)/shard_map/ppermute | solution.py:82
  29.3 18.1 %collective-permute-start.3 = (f32[2,16,256]{2,1,0:T(8,128)S(1)}, f32[2,16,256]{2,1,0:T(8,128)S(1)}, u32[]{:S(2)}, u32[]{:S(2)}) collective-permute-start(f32[2,16,256]{2,1,0:T(8,128)S(1)} %fusion.52), channel_id=1, source_target_pairs={{0,512},{32,544},{64,576},{96,608},{128,640},{160,672},{192,704},{... | collective-permute-start | bytes 98312 | tf_op jit(solution)/shard_map/ppermute | solution.py:82
  30.6 16.8 %collective-permute-start.4 = (f32[2,16,256]{2,1,0:T(8,128)S(1)}, f32[2,16,256]{2,1,0:T(8,128)S(1)}, u32[]{:S(2)}, u32[]{:S(2)}) collective-permute-start(f32[2,16,256]{2,1,0:T(8,128)S(1)} %fusion.52), channel_id=1, source_target_pairs={{0,384},{32,416},{64,448},{96,480},{128,512},{160,544},{192,576},{... | collective-permute-start | bytes 98312 | tf_op jit(solution)/shard_map/ppermute | solution.py:82
  41.8 5.6 %collective-permute-start.5 = (f32[2,16,256]{2,1,0:T(8,128)S(1)}, f32[2,16,256]{2,1,0:T(8,128)S(1)}, u32[]{:S(2)}, u32[]{:S(2)}) collective-permute-start(f32[2,16,256]{2,1,0:T(8,128)S(1)} %fusion.52), channel_id=1, source_target_pairs={{0,256},{32,288},{64,320},{96,352},{128,384},{160,416},{192,448},{... | collective-permute-start | bytes 98312 | tf_op jit(solution)/shard_map/ppermute | solution.py:82
  43.1 4.7 %collective-permute-start.6 = (f32[2,16,256]{2,1,0:T(8,128)S(1)}, f32[2,16,256]{2,1,0:T(8,128)S(1)}, u32[]{:S(2)}, u32[]{:S(2)}) collective-permute-start(f32[2,16,256]{2,1,0:T(8,128)S(1)} %fusion.52), channel_id=1, source_target_pairs={{0,128},{32,160},{64,192},{96,224},{128,256},{160,288},{192,320},{... | collective-permute-start | bytes 98312 | tf_op jit(solution)/shard_map/ppermute | solution.py:82
  46.7 7.4 %collective-permute-start.7 = (f32[8,16,256]{2,1,0:T(8,128)}, f32[8,16,256]{2,1,0:T(8,128)S(1)}, u32[]{:S(2)}, u32[]{:S(2)}) collective-permute-start(f32[8,16,256]{2,1,0:T(8,128)} %bitcast.225), channel_id=1, source_target_pairs={{96,128},{224,256},{352,384},{480,512},{608,640},{736,768},{864,89... | collective-permute-start | bytes 393224 | tf_op jit(solution)/shard_map/ppermute | solution.py:67
  54.3 7.1 %collective-permute-start.8 = (f32[5,8,2,256]{3,2,1,0:T(2,128)S(1)}, f32[5,8,2,256]{3,2,1,0:T(2,128)S(1)}, u32[]{:S(2)}, u32[]{:S(2)}) collective-permute-start(f32[5,8,2,256]{3,2,1,0:T(2,128)S(1)} %get-tuple-element.74), channel_id=1, source_target_pairs={{0,8},{8,16},{16,24},{1,9},{9,17},{17,25},{2,10},{10,18},{18,26},{... | collective-permute-start | bytes 245768 | tf_op jit(solution)/shard_map/ppermute | solution.py:119
  57.7 6.3 %collective-permute-start.9 = (f32[5,8,2,256]{3,2,1,0:T(2,128)S(1)}, f32[5,8,2,256]{3,2,1,0:T(2,128)S(1)}, u32[]{:S(2)}, u32[]{:S(2)}) collective-permute-start(f32[5,8,2,256]{3,2,1,0:T(2,128)S(1)} %get-tuple-element.75), channel_id=1, source_target_pairs={{8,0},{16,8},{24,16},{9,1},{17,9},{25,17},{10,2},{18,10},{26,18},{... | collective-permute-start | bytes 245768 | tf_op jit(solution)/shard_map/ppermute | solution.py:120
  61.4 2.9 %copy-start.8 = (f32[8]{0:T(128)S(1)}, f32[8]{0:T(128)}, u32[]{:S(2)}) copy-start(f32[8]{0:T(128)} %constant.249) | copy-start | bytes 100
  66.7 1.0 %copy-start.7 = (f32[8]{0:T(128)S(1)}, f32[8]{0:T(128)}, u32[]{:S(2)}) copy-start(f32[8]{0:T(128)} %param.12) | copy-start | bytes 100
  70.9 1.2 %copy-start.5 = (f32[8,20,256]{2,1,0:T(8,128)S(1)}, f32[8,20,256]{2,1,0:T(8,128)}, u32[]{:S(2)}) copy-start(f32[8,20,256]{2,1,0:T(8,128)} %get-tuple-element.50) | copy-start | bytes 491524
  72.1 0.9 %copy-start.4 = (f32[8,20,256]{2,1,0:T(8,128)S(1)}, f32[8,20,256]{2,1,0:T(8,128)}, u32[]{:S(2)}) copy-start(f32[8,20,256]{2,1,0:T(8,128)} %get-tuple-element.49) | copy-start | bytes 491524
  72.3 1.0 %copy-start.3 = (f32[8,20,256]{2,1,0:T(8,128)S(1)}, f32[8,20,256]{2,1,0:T(8,128)}, u32[]{:S(2)}) copy-start(f32[8,20,256]{2,1,0:T(8,128)} %get-tuple-element.48) | copy-start | bytes 491524
  73.2 0.9 %copy-start.2 = (f32[8,20,256]{2,1,0:T(8,128)S(1)}, f32[8,20,256]{2,1,0:T(8,128)}, u32[]{:S(2)}) copy-start(f32[8,20,256]{2,1,0:T(8,128)} %get-tuple-element.47) | copy-start | bytes 491524
  74.8 0.7 copy-start.10
  78.9 0.6 copy-start.9
  82.1 2.4 %copy-start.6 = (f32[8,16,256]{2,1,0:T(8,128)S(1)}, f32[8,16,256]{2,1,0:T(8,128)}, u32[]{:S(2)}) copy-start(f32[8,16,256]{2,1,0:T(8,128)} %param.8) | copy-start | bytes 393220

commit v2 on v1

v2 whole, which is shorter than its diff:
```python
import jax
import jax.numpy as jnp
import numpy as np
from jax import lax
from jax.experimental import pallas as pl
from jax.experimental.pallas import tpu as pltpu
from jax.sharding import PartitionSpec as P

NZ = 16
TEAM = 4
time_step = 0.05


def quadrature(node_count):
    points = [(position + 1.0) / node_count for position in range(node_count)]
    weights_table = np.zeros((node_count, node_count))
    for column in range(node_count):
        coeffs = [1.0]
        denominator = 1.0
        for other_node in range(node_count):
            if other_node != column:
                shifted = [0.0] + coeffs
                for degree in range(len(coeffs)):
                    shifted[degree] = shifted[degree] - points[other_node] * coeffs[degree]
                coeffs = shifted
                denominator = denominator * (points[column] - points[other_node])
        for row_node in range(node_count):
            running = 0.0
            for degree in range(len(coeffs)):
                running = running + coeffs[degree] * points[row_node] ** (degree + 1) / (degree + 1)
            weights_table[row_node, column] = running / denominator
    return (weights_table, np.array(points))


def total(terms):
    terms = list(terms)
    while len(terms) > 1:
        terms = [sum(terms[i : i + 2]) for i in range(0, len(terms), 2)]
    return terms[0]


def stencil(s, diff_ref, vel_ref, shape):
    rows, cells = shape
    d, vx, vy, vz = diff_ref[s], 0.5 * vel_ref[0, s], 0.5 * vel_ref[1, s], 0.5 * vel_ref[2, s]
    depth = lax.broadcasted_iota(jnp.int32, shape, 1) % NZ
    up = jnp.where(depth == NZ - 1, 0.0, d - vz)
    down = jnp.where(depth == 0, 0.0, d + vz)

    def apply(v, x_plus, x_minus, decay):
        y_plus = pltpu.roll(v, cells - NZ, 1)
        y_minus = pltpu.roll(v, NZ, 1)
        z_plus = pltpu.roll(v, cells - 1, 1)
        z_minus = pltpu.roll(v, 1, 1)
        return total(
            [
                (d - vx) * x_plus,
                (d + vx) * x_minus,
                (d - vy) * y_plus,
                (d + vy) * y_minus,
                up * z_plus,
                down * z_minus,
                (-6.0 * d - decay) * v,
            ]
        )

    return apply


def coupling(s, v_ref, j, mix_ref):
    return jnp.tanh(total(mix_ref[s, t] * v_ref[j, t] for t in range(v_ref.shape[1])))


def node_starts(s, points, start, force, decay, v_ref):
    for j, tau in enumerate(points):
        step = float(tau * time_step)
        v_ref[j, s] = (start + step * force) / (1.0 + step * decay)


def node_rates(s, v_ref, force, decay, mix_ref, apply):
    rows = v_ref.shape[2]
    out = []
    for j in range(v_ref.shape[0]):
        v = v_ref[j, s]
        moved = apply(v, pltpu.roll(v, rows - 1, 0), pltpu.roll(v, 1, 0), decay)
        out.append(moved + (coupling(s, v_ref, j, mix_ref) + force))
    return out


def swept(m, weights, points, rates, base, v, decay):
    count = len(rates)
    summed = total(float(time_step * weights[m, j]) * rates[j] for j in range(count))
    stiff = float(time_step * points[m] / count) * decay
    return (base + summed + stiff * v) / (1.0 + stiff)


def first_sweep(start_ref, before_ref, force_ref, force_before_ref, decay_ref, mix_ref, diff_ref,
                vel_ref, v_ref, w_ref, v1_ref, handed_ref):
    species, rows, cells = start_ref.shape
    count = v_ref.shape[0]
    weights, points = quadrature(count)

    def begin(s, carry):
        decay = decay_ref[s]
        node_starts(s, points, start_ref[s], force_ref[s], decay, v_ref)
        node_starts(s, points, before_ref[s], force_before_ref[s], decay, w_ref)
        return carry

    lax.fori_loop(0, species, begin, 0)

    def sweep(s, carry):
        decay = decay_ref[s]
        apply = stencil(s, diff_ref, vel_ref, (rows, cells))
        rates = node_rates(s, v_ref, force_ref[s], decay, mix_ref, apply)
        for m in range(count):
            v1_ref[m, s] = swept(m, weights, points, rates, start_ref[s], v_ref[m, s], decay)
        return carry

    lax.fori_loop(0, species, sweep, 0)

    def sweep_before(s, carry):
        decay = decay_ref[s]
        apply = stencil(s, diff_ref, vel_ref, (rows, cells))
        rates = node_rates(s, w_ref, force_before_ref[s], decay, mix_ref, apply)
        m = count - 1
        handed_ref[s] = swept(m, weights, points, rates, before_ref[s], w_ref[m, s], decay)
        return carry

    lax.fori_loop(0, species, sweep_before, 0)


def inner_kernel(start_ref, before_ref, force_ref, force_before_ref, decay_ref, mix_ref, diff_ref,
                 vel_ref, v1_ref, handed_ref, v_ref, w_ref):
    first_sweep(start_ref, before_ref, force_ref, force_before_ref, decay_ref, mix_ref, diff_ref,
                vel_ref, v_ref, w_ref, v1_ref, handed_ref)


def start_kernel(place_ref, base_ref, gathered_ref, handover_ref, force_ref, decay_ref, start_ref,
                 before_ref, force_before_ref, low_ref, high_ref):
    member = place_ref[0]
    planes = base_ref.shape[1]
    for s in range(base_ref.shape[0]):
        base, decay = base_ref[s], decay_ref[s]
        grow = 1.0 + time_step * decay
        factor = 1.0 / grow
        start = base
        force_before = handover_ref[s]
        before = base * grow - time_step * force_before
        for k in range(TEAM - 1):
            passed = member > k
            force = gathered_ref[k, s]
            before = jnp.where(passed, start, before)
            force_before = jnp.where(passed, force, force_before)
            start = jnp.where(passed, factor * (start + time_step * force), start)
        start_ref[s] = start
        before_ref[s] = before
        force_before_ref[s] = force_before
        for k, field in enumerate((start, before, force_ref[s], force_before, decay)):
            low_ref[k, s] = field[:2]
            high_ref[k, s] = field[planes - 2 :]


def outer_kernel(place_ref, row_ref, start_ref, before_ref, force_ref, force_before_ref, decay_ref,
                 initial_ref, below_ref, above_ref, v1_ref, handed_ref, mix_ref, diff_ref, vel_ref,
                 out_ref, e_ref, v_ref, w_ref, v1e_ref, handede_ref, full_ref):
    node, slot, tile, tiles = place_ref[1], place_ref[2], place_ref[3], place_ref[4]
    species, planes, cells = start_ref.shape
    count = v_ref.shape[0]
    for k, ref in enumerate((start_ref, before_ref, force_ref, force_before_ref, decay_ref)):
        for s in range(species):
            e_ref[k, s, 0:2] = below_ref[k, s]
            e_ref[k, s, 2:4] = ref[s, 0:2]
            e_ref[k, s, 4:6] = ref[s, planes - 2 : planes]
            e_ref[k, s, 6:8] = above_ref[k, s]
    first_sweep(e_ref.at[0], e_ref.at[1], e_ref.at[2], e_ref.at[3], e_ref.at[4], mix_ref, diff_ref,
                vel_ref, v_ref, w_ref, v1e_ref, handede_ref)
    edge = lax.broadcasted_iota(jnp.int32, (8, cells), 0)
    outside = ((tile == 0) & (edge == 1)) | ((tile == tiles - 1) & (edge == 6))
    row = lax.broadcasted_iota(jnp.int32, (planes, cells), 0)

    def fill(s, carry):
        for j in range(count):
            v1e = v1e_ref[j, s]
            v1e_ref[j, s] = jnp.where(outside, 0.0, v1e)
            full_ref[j, s] = v1_ref[j, s]
            full_ref[j, s, 0:1] = v1e[2:3]
            full_ref[j, s, planes - 1 : planes] = v1e[5:6]
        return carry

    lax.fori_loop(0, species, fill, 0)
    scale = float(time_step / count / count)
    stiff_of_node = scale * (node + 1).astype(jnp.float32)

    def finish(s, carry):
        decay = decay_ref[s]
        apply = stencil(s, diff_ref, vel_ref, (planes, cells))
        mixed = total(row_ref[j] * full_ref[j, s] for j in range(count))
        mixed_edge = total(row_ref[j] * v1e_ref[j, s] for j in range(count))
        x_plus = jnp.where(row == planes - 1, mixed_edge[6:7], pltpu.roll(mixed, planes - 1, 0))
        x_minus = jnp.where(row == 0, mixed_edge[1:2], pltpu.roll(mixed, 1, 0))
        coupled = total(row_ref[j] * coupling(s, full_ref, j, mix_ref) for j in range(count))
        weight = total(row_ref[j] for j in range(count))
        summed = apply(mixed, x_plus, x_minus, decay) + coupled + weight * force_ref[s]
        handede = handede_ref[s]
        handed = handed_ref[s]
        handed = jnp.where(row == 0, handede[2:3], handed)
        handed = jnp.where(row == planes - 1, handede[5:6], handed)
        second_start = jnp.where(slot == 0, initial_ref[s], handed)
        stiff = stiff_of_node * decay
        own = full_ref[node, s]
        out_ref[0, 0, s] = (second_start + time_step * summed + stiff * own) / (1.0 + stiff)
        return carry

    lax.fori_loop(0, species, finish, 0)


def call(kernel, outs, ins, scratch, cost):
    spaces = [pltpu.SMEM if kind == "s" else pltpu.VMEM for kind in ins]
    return pl.pallas_call(
        kernel,
        out_shape=[jax.ShapeDtypeStruct(shape, jnp.float32) for shape in outs],
        in_specs=[pl.BlockSpec(memory_space=space) for space in spaces],
        out_specs=[pl.BlockSpec(memory_space=pltpu.VMEM)] * len(outs),
        scratch_shapes=[pltpu.VMEM(shape, jnp.float32) for shape in scratch],
        cost_estimate=pl.CostEstimate(flops=cost, bytes_accessed=cost // 8, transcendentals=0),
        compiler_params=pltpu.CompilerParams(vmem_limit_bytes=24 * 2**20),
    )


def team_base(initial, force, decay_rate):
    slices = lax.axis_size("tm")
    place = lax.axis_index("tm")
    member = place % TEAM
    team = place // TEAM
    teams = slices // TEAM
    groups = [[TEAM * g + i for i in range(TEAM)] for g in range(teams)]
    handover = lax.ppermute(force, "tm", [(TEAM * g - 1, TEAM * g) for g in range(1, teams)])
    gathered = lax.all_gather(force, "tm", axis_index_groups=groups)
    share = force.shape[0] // TEAM

    def own(array, axis):
        return lax.dynamic_slice_in_dim(array, member * share, share, axis)

    factor = 1.0 / (1.0 + time_step * own(decay_rate, 0))
    own_gathered = own(gathered, 1)
    summed = jnp.zeros_like(factor)
    for k in range(TEAM):
        summed = factor * (summed + time_step * own_gathered[k])
    factor2 = factor * factor
    factor4 = factor2 * factor2

    def forward(value, distance, senders):
        pairs = [(TEAM * g + i, TEAM * (g + distance) + i) for g in senders for i in range(TEAM)]
        return lax.ppermute(value, "tm", pairs)

    near = forward(summed, 1, range(teams - 1))
    own_initial = own(initial, 0)
    state = jnp.where(team == 0, own_initial, factor4 * own_initial + near)
    for first in range(0, teams - 2, 2):
        senders = range(first, min(first + 2, teams - 2))
        ahead = forward(factor4 * state + summed, 2, senders)
        reached = (team == first + 2) | (team == first + 3)
        state = jnp.where(reached, factor4 * ahead + near, state)
    base = lax.all_gather(state, "tm", axis=0, tiled=True, axis_index_groups=groups)
    return base, gathered, handover


def body(initial, forcing, decay_rate, mixing, diffusivity, velocity):
    count = lax.axis_size("node")
    node = lax.axis_index("node")
    place = lax.axis_index("tm")
    tiles = lax.axis_size("space")
    tile = lax.axis_index("space")
    force = forcing[0]
    base, gathered, handover = team_base(initial, force, decay_rate)
    where_am_i = jnp.stack([place % TEAM, node, place, tile, jnp.int32(tiles)]).astype(jnp.int32)
    weights = jnp.asarray(quadrature(count)[0], jnp.float32)
    own_row = lax.dynamic_index_in_dim(weights, node, 0, False)

    full = force.shape
    species, planes, cells = full
    edge = (5, species, 2, cells)
    start, before, force_before, low, high = call(
        start_kernel, [full, full, full, edge, edge], "svvvvv", [], 2**20
    )(where_am_i, base, gathered, handover, force, decay_rate)
    up = [(i, i + 1) for i in range(tiles - 1)]
    down = [(j, i) for i, j in up]
    below = lax.ppermute(high, "space", up)
    above = lax.ppermute(low, "space", down)
    nodes = (count,) + full
    params = (mixing, diffusivity, velocity)
    fields = (start, before, force, force_before, decay_rate)
    v1, handed = call(inner_kernel, [nodes, full], "vvvvvsss", [nodes, nodes], 2**25)(
        *fields, *params
    )
    small = (species, 8, cells)
    edges = (count,) + small
    (out,) = call(
        outer_kernel,
        [(1, 1) + full],
        "ss" + "v" * 10 + "sss",
        [(5,) + small, edges, edges, edges, small, nodes],
        2**25,
    )(where_am_i, own_row, *fields, initial, below, above, v1, handed, *params)
    return out


def solution(mesh):
    placed = (
        P(None, "space", None),
        P("tm", None, "space", None),
        P(None, "space", None),
        P(),
        P(),
        P(),
    )
    return jax.shard_map(
        body,
        mesh=mesh,
        in_specs=placed,
        out_specs=P("tm", "node", None, "space", None),
        check_vma=False,
    )
```

time: 86 us -> 60.2 us (0.70)
  the two profiles are of different devices: /device:TPU:50 before, /device:TPU:188 now
where the time goes in v2:
time: 60.2 us; the launch traced here: 59.9 us
  starting transfers between devices  26 us (43%)
  blocking collectives  17.8 us (30%)
  Pallas kernels  11.1 us (18%)
  waiting for transfers between devices  3.14 us (5%)
  local copies, waits for them, and re-layouts  1.48 us (2%)
    ppermute x4, starting transfers between devices, forward(): return lax.ppermute(value, 'tm', pairs)  18.9 us
    all_gather x1, blocking collectives, team_base(): lax.all_gather(state, 'tm', axis=0, tiled=True, axis_index_groups=groups)  9.45 us
    all_gather x1, blocking collectives, team_base(): gathered = lax.all_gather(force, 'tm', axis_index_groups=groups)  8.38 us
    pallas_call x1, Pallas kernels, body(): call(outer_kernel, [(1, 1) + full], 'ss' + 'v' * 10 + 'sss', [(5,) + smal...  5.33 us
    pallas_call x1, Pallas kernels, body(): call(inner_kernel, [nodes, full], 'vvvvvsss', [nodes, nodes], 2 ** 25)  5.05 us
    ppermute x4, waiting for transfers between devices, forward(): return lax.ppermute(value, 'tm', pairs)  3.13 us
    ppermute x1, starting transfers between devices, body(): below = lax.ppermute(high, 'space', up)  3.11 us
    ppermute x1, starting transfers between devices, body(): above = lax.ppermute(low, 'space', down)  2.74 us
  transfers between devices with their start and end apart: 7, of which 2 were waited for; matrix products, arithmetic and copies ran while one was open for 1% of the time, Pallas kernels for 8%

profile of v2, /device:TPU:188, one launch (start us, length us, event | category | flops | bytes accessed | tf_op | source)
XLA Modules:
  0.0 59.9 jit_solution(15306740861093737885)
XLA Ops:
  0.0 0.0 copy-start
  0.0 8.4 %all_gather.6.gathered_ref = f32[4,8,16,256]{3,2,1,0:T(8,128)S(1)} all-gather(f32[1,8,16,256]{3,2,1,0:T(8,128)} %param.8), channel_id=1, replica_groups={{0,32,64,96},{128,160,192,224},{256,288,320,352},{384,416,448,480},{512..., dimensions={0}, use_global_device_ids=true | all-gather | bytes 655360 | tf_op jit(solution)/shard_map/all_gather | solution.py:237
  8.4 0.0 copy-start.2
  8.4 0.0 copy-done
  8.4 7.4 %collective-permute-start = (f32[2,16,256]{2,1,0:T(8,128)S(1)}, f32[2,16,256]{2,1,0:T(8,128)S(1)}, u32[]{:S(2)}, u32[]{:S(2)}) collective-permute-start(f32[2,16,256]{2,1,0:T(8,128)S(1)} %fusion.2), channel_id=1, source_target_pairs={{0,128},{32,160},{64,192},{96,224},{128,256},{160,288},{192,320},{... | collective-permute-start | bytes 98312 | tf_op jit(solution)/shard_map/ppermute | solution.py:253
  15.9 1.6 %collective-permute-done = f32[2,16,256]{2,1,0:T(8,128)S(1)} collective-permute-done((f32[2,16,256]{2,1,0:T(8,128)S(1)}, f32[2,16,256]{2,1,0:T(8,128)S(1)}, u32[]{:S(2)}, u32[]{:S(2)}) %collective-permute-start) | collective-permute-done | bytes 32800 | tf_op jit(solution)/shard_map/ppermute | solution.py:253
  17.4 0.0 copy-done.2
  17.5 10.0 %collective-permute-start.1 = (f32[2,16,256]{2,1,0:T(8,128)S(1)}, f32[2,16,256]{2,1,0:T(8,128)S(1)}, u32[]{:S(2)}, u32[]{:S(2)}) collective-permute-start(f32[2,16,256]{2,1,0:T(8,128)S(1)} %multiply_add_fusion.2), channel_id=1, source_target_pairs={{0,256},{32,288},{64,320},{96,352},{128,384},{160,416},{192,448},{... | collective-permute-start | bytes 98312 | tf_op jit(solution)/shard_map/ppermute | solution.py:253
  27.5 1.6 %collective-permute-done.1 = f32[2,16,256]{2,1,0:T(8,128)S(1)} collective-permute-done((f32[2,16,256]{2,1,0:T(8,128)S(1)}, f32[2,16,256]{2,1,0:T(8,128)S(1)}, u32[]{:S(2)}, u32[]{:S(2)}) %collective-permute-start.1) | collective-permute-done | bytes 32800 | tf_op jit(solution)/shard_map/ppermute | solution.py:253
  29.1 0.0 copy-start.1
  29.1 0.8 %collective-permute-start.2 = (f32[2,16,256]{2,1,0:T(8,128)S(1)}, f32[2,16,256]{2,1,0:T(8,128)S(1)}, u32[]{:S(2)}, u32[]{:S(2)}) collective-permute-start(f32[2,16,256]{2,1,0:T(8,128)S(1)} %multiply_add_fusion.1), channel_id=1, source_target_pairs={{256,512},{288,544},{320,576},{352,608},{384,640},{416,672},{448,7... | collective-permute-start | bytes 98312 | tf_op jit(solution)/shard_map/ppermute | solution.py:253
  29.9 0.0 collective-permute-done.2
  30.0 0.7 %collective-permute-start.3 = (f32[2,16,256]{2,1,0:T(8,128)S(1)}, f32[2,16,256]{2,1,0:T(8,128)S(1)}, u32[]{:S(2)}, u32[]{:S(2)}) collective-permute-start(f32[2,16,256]{2,1,0:T(8,128)S(1)} %multiply_add_fusion), channel_id=1, source_target_pairs={{512,768},{544,800},{576,832},{608,864},{640,896},{672,928},{704,9... | collective-permute-start | bytes 98312 | tf_op jit(solution)/shard_map/ppermute | solution.py:253
  30.6 0.0 copy-done.1
  30.7 1.3 %collective-permute-start.4 = (f32[8,16,256]{2,1,0:T(8,128)S(1)}, f32[8,16,256]{2,1,0:T(8,128)S(1)}, u32[]{:S(2)}, u32[]{:S(2)}) collective-permute-start(f32[8,16,256]{2,1,0:T(8,128)S(1)} %bitcast.35), channel_id=1, source_target_pairs={{96,128},{224,256},{352,384},{480,512},{608,640},{736,768},{864,89... | collective-permute-start | bytes 393224 | tf_op jit(solution)/shard_map/ppermute | solution.py:236
  32.0 0.1 stack.19.place_ref
  32.1 0.0 collective-permute-done.3
  32.1 9.5 %all_gather.7.base_ref = f32[8,16,256]{2,1,0:T(8,128)S(1)} all-gather(f32[2,16,256]{2,1,0:T(8,128)S(1)} %add_select_fusion), channel_id=1, replica_groups={{0,32,64,96},{128,160,192,224},{256,288,320,352},{384,416,448,480},{512..., dimensions={0}, use_global_device_ids=true | all-gather | bytes 163840 | tf_op jit(solution)/shard_map/all_gather | solution.py:263
  41.5 0.0 collective-permute-done.4.handover_ref
  41.6 0.7 %shard_map.73 = (f32[8,16,256]{2,1,0:T(8,128)S(1)}, f32[8,16,256]{2,1,0:T(8,128)S(1)}, f32[8,16,256]{2,1,0:T(8,128)S(1)}, f32[5,8,2,256]{3,2,1,0:T(2,128)S(1)}, f32[5,8,2,256]{3,2,1,0:T(2,128)S(1)}) custom-call(s32[5]{0:T(128)S(1)} %stack.19.place_ref, f32[8,16,256]{2,1,0:T(8,128)S(1)} %all_gather.7.base_ref, f32[4,8,16,256]{3,2,1,0:T(8,128)S(1)} %all_gather.6.gathered_ref, ...), custom_call_target="tpu_custom_call" | custom-call | flops 1048576 | bytes 131072 | tf_op jit(solution)/shard_map/pallas_call | solution.py:282
  42.2 3.1 %collective-permute-start.5 = (f32[5,8,2,256]{3,2,1,0:T(2,128)S(1)}, f32[5,8,2,256]{3,2,1,0:T(2,128)S(1)}, u32[]{:S(2)}, u32[]{:S(2)}) collective-permute-start(f32[5,8,2,256]{3,2,1,0:T(2,128)S(1)} %get-tuple-element.15), channel_id=1, source_target_pairs={{0,8},{8,16},{16,24},{1,9},{9,17},{17,25},{2,10},{10,18},{18,26},{... | collective-permute-start | bytes 245768 | tf_op jit(solution)/shard_map/ppermute | solution.py:287
  45.3 0.0 copy-start.3
  45.4 2.7 %collective-permute-start.6 = (f32[5,8,2,256]{3,2,1,0:T(2,128)S(1)}, f32[5,8,2,256]{3,2,1,0:T(2,128)S(1)}, u32[]{:S(2)}, u32[]{:S(2)}) collective-permute-start(f32[5,8,2,256]{3,2,1,0:T(2,128)S(1)} %get-tuple-element.16), channel_id=1, source_target_pairs={{8,0},{16,8},{24,16},{9,1},{17,9},{25,17},{10,2},{18,10},{26,18},{... | collective-permute-start | bytes 245768 | tf_op jit(solution)/shard_map/ppermute | solution.py:288
  48.1 0.7 %fusion.11.row_ref = f32[8]{0:T(128)S(1)} fusion(f32[8,8]{1,0:T(8,128)} %constant.64.clone, s32[]{:T(128)S(6)} %select_n.49), kind=kLoop, calls=%fused_computation.25 | loop fusion | bytes 68 | tf_op jit(solution)/shard_map/jit(dynamic_index_in_dim)/squeeze | solution.py:277
  48.8 0.0 copy-start.4
  48.8 0.0 copy-start.5
  48.8 0.0 copy-done.3
  48.8 0.7 %copy-done.4 = f32[3,8]{1,0:T(4,128)S(1)} copy-done((f32[3,8]{1,0:T(4,128)S(1)}, f32[3,8]{1,0:T(4,128)}, u32[]{:S(2)}) %copy-start.4) | copy-done | bytes 120
  49.5 0.0 copy-done.5
  49.5 5.0 %shard_map.74 = (f32[8,8,16,256]{3,2,1,0:T(8,128)S(1)}, f32[8,16,256]{2,1,0:T(8,128)S(1)}) custom-call(f32[8,16,256]{2,1,0:T(8,128)S(1)} %get-tuple-element.12.start_ref, f32[8,16,256]{2,1,0:T(8,128)S(1)} %get-tuple-element.13.before_ref, f32[8,16,256]{2,1,0:T(8,128)S(1)} %bitcast.37, f32[8,16,256]{2,1,0:T(8,128)S(1)} %get-tuple-element.14.force_before_ref, ...), custom_call_target="tpu_custom_call" | custom-call | flops 33554432 | bytes 4194304 | tf_op jit(solution)/shard_map/pallas_call | solution.py:292
  54.5 0.0 collective-permute-done.5.below_ref
  54.6 0.0 collective-permute-done.6.above_ref
  54.6 5.3 %shard_map.75 = f32[1,1,8,16,256]{4,3,2,1,0:T(8,128)} custom-call(s32[5]{0:T(128)S(1)} %stack.19.place_ref, f32[8]{0:T(128)S(1)} %fusion.11.row_ref, f32[8,16,256]{2,1,0:T(8,128)S(1)} %get-tuple-element.12.start_ref, f32[8,16,256]{2,1,0:T(8,128)S(1)} %get-tuple-element.13.before_ref, f32[8,16,256]{2,1,0:T(8,128)S(1)} %bitcast.38, ...), custom_call_target="tpu_custom_call" | custom-call | flops 33554432 | bytes 4194304 | tf_op jit(solution)/shard_map/pallas_call | solution.py:297
  (5 shorter events, 0.1 us)
Async XLA Ops:
  0.0 8.4 %copy-start = (f32[8,16,256]{2,1,0:T(8,128)S(1)}, f32[8,16,256]{2,1,0:T(8,128)}, u32[]{:S(2)}) copy-start(f32[8,16,256]{2,1,0:T(8,128)} %decay_ref.5) | copy-start | bytes 393220
  8.4 9.1 %copy-start.2 = (f32[8,16,256]{2,1,0:T(8,128)S(1)}, f32[8,16,256]{2,1,0:T(8,128)}, u32[]{:S(2)}) copy-start(f32[8,16,256]{2,1,0:T(8,128)} %initial_ref.1) | copy-start | bytes 393220
  8.4 9.0 %collective-permute-start = (f32[2,16,256]{2,1,0:T(8,128)S(1)}, f32[2,16,256]{2,1,0:T(8,128)S(1)}, u32[]{:S(2)}, u32[]{:S(2)}) collective-permute-start(f32[2,16,256]{2,1,0:T(8,128)S(1)} %fusion.2), channel_id=1, source_target_pairs={{0,128},{32,160},{64,192},{96,224},{128,256},{160,288},{192,320},{... | collective-permute-start | bytes 98312 | tf_op jit(solution)/shard_map/ppermute | solution.py:253
  17.5 11.6 %collective-permute-start.1 = (f32[2,16,256]{2,1,0:T(8,128)S(1)}, f32[2,16,256]{2,1,0:T(8,128)S(1)}, u32[]{:S(2)}, u32[]{:S(2)}) collective-permute-start(f32[2,16,256]{2,1,0:T(8,128)S(1)} %multiply_add_fusion.2), channel_id=1, source_target_pairs={{0,256},{32,288},{64,320},{96,352},{128,384},{160,416},{192,448},{... | collective-permute-start | bytes 98312 | tf_op jit(solution)/shard_map/ppermute | solution.py:253
  29.1 1.6 %copy-start.1 = (f32[1,8,16,256]{3,2,1,0:T(8,128)S(1)}, f32[1,8,16,256]{3,2,1,0:T(8,128)}, u32[]{:S(2)}) copy-start(f32[1,8,16,256]{3,2,1,0:T(8,128)} %param.8) | copy-start | bytes 393220
  29.1 0.8 %collective-permute-start.2 = (f32[2,16,256]{2,1,0:T(8,128)S(1)}, f32[2,16,256]{2,1,0:T(8,128)S(1)}, u32[]{:S(2)}, u32[]{:S(2)}) collective-permute-start(f32[2,16,256]{2,1,0:T(8,128)S(1)} %multiply_add_fusion.1), channel_id=1, source_target_pairs={{256,512},{288,544},{320,576},{352,608},{384,640},{416,672},{448,7... | collective-permute-start | bytes 98312 | tf_op jit(solution)/shard_map/ppermute | solution.py:253
  30.0 2.1 %collective-permute-start.3 = (f32[2,16,256]{2,1,0:T(8,128)S(1)}, f32[2,16,256]{2,1,0:T(8,128)S(1)}, u32[]{:S(2)}, u32[]{:S(2)}) collective-permute-start(f32[2,16,256]{2,1,0:T(8,128)S(1)} %multiply_add_fusion), channel_id=1, source_target_pairs={{512,768},{544,800},{576,832},{608,864},{640,896},{672,928},{704,9... | collective-permute-start | bytes 98312 | tf_op jit(solution)/shard_map/ppermute | solution.py:253
  30.7 10.9 %collective-permute-start.4 = (f32[8,16,256]{2,1,0:T(8,128)S(1)}, f32[8,16,256]{2,1,0:T(8,128)S(1)}, u32[]{:S(2)}, u32[]{:S(2)}) collective-permute-start(f32[8,16,256]{2,1,0:T(8,128)S(1)} %bitcast.35), channel_id=1, source_target_pairs={{96,128},{224,256},{352,384},{480,512},{608,640},{736,768},{864,89... | collective-permute-start | bytes 393224 | tf_op jit(solution)/shard_map/ppermute | solution.py:236
  42.2 12.3 %collective-permute-start.5 = (f32[5,8,2,256]{3,2,1,0:T(2,128)S(1)}, f32[5,8,2,256]{3,2,1,0:T(2,128)S(1)}, u32[]{:S(2)}, u32[]{:S(2)}) collective-permute-start(f32[5,8,2,256]{3,2,1,0:T(2,128)S(1)} %get-tuple-element.15), channel_id=1, source_target_pairs={{0,8},{8,16},{16,24},{1,9},{9,17},{17,25},{2,10},{10,18},{18,26},{... | collective-permute-start | bytes 245768 | tf_op jit(solution)/shard_map/ppermute | solution.py:287
  45.3 3.5 %copy-start.3 = (f32[8,8]{1,0:T(8,128)S(1)}, f32[8,8]{1,0:T(8,128)}, u32[]{:S(2)}) copy-start(f32[8,8]{1,0:T(8,128)} %mix_ref.3) | copy-start | bytes 772
  45.4 9.2 %collective-permute-start.6 = (f32[5,8,2,256]{3,2,1,0:T(2,128)S(1)}, f32[5,8,2,256]{3,2,1,0:T(2,128)S(1)}, u32[]{:S(2)}, u32[]{:S(2)}) collective-permute-start(f32[5,8,2,256]{3,2,1,0:T(2,128)S(1)} %get-tuple-element.16), channel_id=1, source_target_pairs={{8,0},{16,8},{24,16},{9,1},{17,9},{25,17},{10,2},{18,10},{26,18},{... | collective-permute-start | bytes 245768 | tf_op jit(solution)/shard_map/ppermute | solution.py:288
  48.8 0.7 %copy-start.4 = (f32[3,8]{1,0:T(4,128)S(1)}, f32[3,8]{1,0:T(4,128)}, u32[]{:S(2)}) copy-start(f32[3,8]{1,0:T(4,128)} %vel_ref.3) | copy-start | bytes 292
  48.8 0.7 %copy-start.5 = (f32[8]{0:T(128)S(1)}, f32[8]{0:T(128)}, u32[]{:S(2)}) copy-start(f32[8]{0:T(128)} %diff_ref.3) | copy-start | bytes 100

commit v3 on v2

--- a/solution.py
+++ b/solution.py
@@ -33,10 +33,10 @@
 
 
 def total(terms):
-    terms = list(terms)
-    while len(terms) > 1:
-        terms = [sum(terms[i : i + 2]) for i in range(0, len(terms), 2)]
-    return terms[0]
+    out = None
+    for term in terms:
+        out = term if out is None else out + term
+    return out
 
 
 def stencil(s, diff_ref, vel_ref, shape):
@@ -70,10 +70,12 @@
     return jnp.tanh(total(mix_ref[s, t] * v_ref[j, t] for t in range(v_ref.shape[1])))
 
 
-def node_starts(s, points, start, force, decay, v_ref):
+def node_starts(s, points, fields, decay):
     for j, tau in enumerate(points):
         step = float(tau * time_step)
-        v_ref[j, s] = (start + step * force) / (1.0 + step * decay)
+        shrink = 1.0 / (1.0 + step * decay)
+        for start, force, v_ref in fields:
+            v_ref[j, s] = (start + step * force) * shrink
 
 
 def node_rates(s, v_ref, force, decay, mix_ref, apply):
@@ -94,18 +96,21 @@
 
 
 def first_sweep(start_ref, before_ref, force_ref, force_before_ref, decay_ref, mix_ref, diff_ref,
-                vel_ref, v_ref, w_ref, v1_ref, handed_ref):
+                vel_ref, v_ref, w_ref, v1_ref, handed_ref, ready):
     species, rows, cells = start_ref.shape
     count = v_ref.shape[0]
     weights, points = quadrature(count)
 
     def begin(s, carry):
         decay = decay_ref[s]
-        node_starts(s, points, start_ref[s], force_ref[s], decay, v_ref)
-        node_starts(s, points, before_ref[s], force_before_ref[s], decay, w_ref)
-        return carry
-
-    lax.fori_loop(0, species, begin, 0)
+        now = (start_ref[s], force_ref[s], v_ref)
+        then = (before_ref[s], force_before_ref[s], w_ref)
+        node_starts(s, points, (now, then), decay)
+        return carry
+
+    lax.fori_loop(0, species, begin, 0, unroll=4)
+
+    ready()
 
     def sweep(s, carry):
         decay = decay_ref[s]
@@ -115,23 +120,41 @@
             v1_ref[m, s] = swept(m, weights, points, rates, start_ref[s], v_ref[m, s], decay)
         return carry
 
-    lax.fori_loop(0, species, sweep, 0)
+    lax.fori_loop(0, species, sweep, 0, unroll=4)
 
     def sweep_before(s, carry):
         decay = decay_ref[s]
         apply = stencil(s, diff_ref, vel_ref, (rows, cells))
-        rates = node_rates(s, w_ref, force_before_ref[s], decay, mix_ref, apply)
         m = count - 1
-        handed_ref[s] = swept(m, weights, points, rates, before_ref[s], w_ref[m, s], decay)
-        return carry
-
-    lax.fori_loop(0, species, sweep_before, 0)
-
-
-def inner_kernel(start_ref, before_ref, force_ref, force_before_ref, decay_ref, mix_ref, diff_ref,
-                 vel_ref, v1_ref, handed_ref, v_ref, w_ref):
+        row = [float(time_step * weights[m, j]) for j in range(count)]
+        mixed = total(row[j] * w_ref[j, s] for j in range(count))
+        coupled = total(row[j] * coupling(s, w_ref, j, mix_ref) for j in range(count))
+        moved = apply(mixed, pltpu.roll(mixed, rows - 1, 0), pltpu.roll(mixed, 1, 0), decay)
+        stiff = float(time_step * points[m] / count) * decay
+        base = before_ref[s] + float(sum(row)) * force_before_ref[s]
+        handed_ref[s] = (base + (moved + coupled) + stiff * w_ref[m, s]) / (1.0 + stiff)
+        return carry
+
+    lax.fori_loop(0, species, sweep_before, 0, unroll=4)
+
+
+def fetch(sources, targets, sems):
+    copies = [pltpu.make_async_copy(a, b, sems.at[i]) for i, (a, b) in enumerate(zip(sources, targets))]
+    for copy in copies:
+        copy.start()
+
+    def ready():
+        for copy in copies:
+            copy.wait()
+
+    return ready
+
+
+def inner_kernel(start_ref, before_ref, force_ref, force_before_ref, decay_ref, mix_hbm, diff_hbm,
+                 vel_hbm, v1_ref, handed_ref, v_ref, w_ref, mix_ref, diff_ref, vel_ref, sems):
+    ready = fetch((mix_hbm, diff_hbm, vel_hbm), (mix_ref, diff_ref, vel_ref), sems)
     first_sweep(start_ref, before_ref, force_ref, force_before_ref, decay_ref, mix_ref, diff_ref,
-                vel_ref, v_ref, w_ref, v1_ref, handed_ref)
+                vel_ref, v_ref, w_ref, v1_ref, handed_ref, ready)
 
 
 def start_kernel(place_ref, base_ref, gathered_ref, handover_ref, force_ref, decay_ref, start_ref,
@@ -159,9 +182,11 @@
             high_ref[k, s] = field[planes - 2 :]
 
 
-def outer_kernel(place_ref, row_ref, start_ref, before_ref, force_ref, force_before_ref, decay_ref,
-                 initial_ref, below_ref, above_ref, v1_ref, handed_ref, mix_ref, diff_ref, vel_ref,
-                 out_ref, e_ref, v_ref, w_ref, v1e_ref, handede_ref, full_ref):
+def outer_kernel(place_ref, start_ref, before_ref, force_ref, force_before_ref, decay_ref,
+                 initial_ref, below_ref, above_ref, v1_ref, handed_ref, mix_hbm, diff_hbm, vel_hbm,
+                 out_ref, e_ref, v_ref, w_ref, v1e_ref, handede_ref, full_ref, mix_ref, diff_ref,
+                 vel_ref, sems):
+    ready = fetch((mix_hbm, diff_hbm, vel_hbm), (mix_ref, diff_ref, vel_ref), sems)
     node, slot, tile, tiles = place_ref[1], place_ref[2], place_ref[3], place_ref[4]
     species, planes, cells = start_ref.shape
     count = v_ref.shape[0]
@@ -172,7 +197,7 @@
             e_ref[k, s, 4:6] = ref[s, planes - 2 : planes]
             e_ref[k, s, 6:8] = above_ref[k, s]
     first_sweep(e_ref.at[0], e_ref.at[1], e_ref.at[2], e_ref.at[3], e_ref.at[4], mix_ref, diff_ref,
-                vel_ref, v_ref, w_ref, v1e_ref, handede_ref)
+                vel_ref, v_ref, w_ref, v1e_ref, handede_ref, ready)
     edge = lax.broadcasted_iota(jnp.int32, (8, cells), 0)
     outside = ((tile == 0) & (edge == 1)) | ((tile == tiles - 1) & (edge == 6))
     row = lax.broadcasted_iota(jnp.int32, (planes, cells), 0)
@@ -186,19 +211,26 @@
             full_ref[j, s, planes - 1 : planes] = v1e[5:6]
         return carry
 
-    lax.fori_loop(0, species, fill, 0)
+    lax.fori_loop(0, species, fill, 0, unroll=4)
+    weights = quadrature(count)[0]
+    own_row = []
+    for j in range(count):
+        weight = jnp.float32(weights[0, j])
+        for m in range(1, count):
+            weight = jnp.where(node == m, jnp.float32(weights[m, j]), weight)
+        own_row.append(weight)
     scale = float(time_step / count / count)
     stiff_of_node = scale * (node + 1).astype(jnp.float32)
 
     def finish(s, carry):
         decay = decay_ref[s]
         apply = stencil(s, diff_ref, vel_ref, (planes, cells))
-        mixed = total(row_ref[j] * full_ref[j, s] for j in range(count))
-        mixed_edge = total(row_ref[j] * v1e_ref[j, s] for j in range(count))
+        mixed = total(own_row[j] * full_ref[j, s] for j in range(count))
+        mixed_edge = total(own_row[j] * v1e_ref[j, s] for j in range(count))
         x_plus = jnp.where(row == planes - 1, mixed_edge[6:7], pltpu.roll(mixed, planes - 1, 0))
         x_minus = jnp.where(row == 0, mixed_edge[1:2], pltpu.roll(mixed, 1, 0))
-        coupled = total(row_ref[j] * coupling(s, full_ref, j, mix_ref) for j in range(count))
-        weight = total(row_ref[j] for j in range(count))
+        coupled = total(own_row[j] * coupling(s, full_ref, j, mix_ref) for j in range(count))
+        weight = total(own_row[j] for j in range(count))
         summed = apply(mixed, x_plus, x_minus, decay) + coupled + weight * force_ref[s]
         handede = handede_ref[s]
         handed = handed_ref[s]
@@ -210,17 +242,21 @@
         out_ref[0, 0, s] = (second_start + time_step * summed + stiff * own) / (1.0 + stiff)
         return carry
 
-    lax.fori_loop(0, species, finish, 0)
-
-
-def call(kernel, outs, ins, scratch, cost):
-    spaces = [pltpu.SMEM if kind == "s" else pltpu.VMEM for kind in ins]
+    lax.fori_loop(0, species, finish, 0, unroll=4)
+
+
+def call(kernel, outs, ins, scratch, cost, params=()):
+    spaces = [{"s": pltpu.SMEM, "v": pltpu.VMEM, "h": pltpu.HBM}[kind] for kind in ins]
+    scratch = [pltpu.VMEM(shape, jnp.float32) for shape in scratch]
+    if "h" in ins:
+        scratch += [pltpu.SMEM(shape, jnp.float32) for shape in params]
+        scratch += [pltpu.SemaphoreType.DMA((len(params),))]
     return pl.pallas_call(
         kernel,
         out_shape=[jax.ShapeDtypeStruct(shape, jnp.float32) for shape in outs],
         in_specs=[pl.BlockSpec(memory_space=space) for space in spaces],
         out_specs=[pl.BlockSpec(memory_space=pltpu.VMEM)] * len(outs),
-        scratch_shapes=[pltpu.VMEM(shape, jnp.float32) for shape in scratch],
+        scratch_shapes=scratch,
         cost_estimate=pl.CostEstimate(flops=cost, bytes_accessed=cost // 8, transcendentals=0),
         compiler_params=pltpu.CompilerParams(vmem_limit_bytes=24 * 2**20),
     )
@@ -248,18 +284,25 @@
     factor2 = factor * factor
     factor4 = factor2 * factor2
 
-    def forward(value, distance, senders):
-        pairs = [(TEAM * g + i, TEAM * (g + distance) + i) for g in senders for i in range(TEAM)]
+    def send(value, *routes):
+        pairs = [(TEAM * g + i, TEAM * t + i) for g, t in routes for i in range(TEAM)]
         return lax.ppermute(value, "tm", pairs)
 
-    near = forward(summed, 1, range(teams - 1))
-    own_initial = own(initial, 0)
-    state = jnp.where(team == 0, own_initial, factor4 * own_initial + near)
-    for first in range(0, teams - 2, 2):
-        senders = range(first, min(first + 2, teams - 2))
-        ahead = forward(factor4 * state + summed, 2, senders)
-        reached = (team == first + 2) | (team == first + 3)
-        state = jnp.where(reached, factor4 * ahead + near, state)
+    middle = teams // 2 - 1
+    near = send(summed, *((g, g + 1) for g in range(middle + 1, teams - 1, 2)))
+    state = own(initial, 0)
+    for g in range(middle):
+        arrived = send(factor4 * state + summed, (g, g + 1))
+        state = jnp.where(team == g + 1, arrived, state)
+    waiting = []
+    for g in range(middle, teams, 2):
+        routes = waiting + ([(g, g + 2)] if g + 2 < teams else [])
+        if routes:
+            arrived = send(factor4 * state + summed, *routes)
+            for _, t in waiting:
+                state = jnp.where(team == t, arrived, state)
+            state = jnp.where(team == g + 2, factor4 * arrived + near, state)
+        waiting = [(g, g + 1)] if g + 1 < teams else []
     base = lax.all_gather(state, "tm", axis=0, tiled=True, axis_index_groups=groups)
     return base, gathered, handover
 
@@ -273,9 +316,6 @@
     force = forcing[0]
     base, gathered, handover = team_base(initial, force, decay_rate)
     where_am_i = jnp.stack([place % TEAM, node, place, tile, jnp.int32(tiles)]).astype(jnp.int32)
-    weights = jnp.asarray(quadrature(count)[0], jnp.float32)
-    own_row = lax.dynamic_index_in_dim(weights, node, 0, False)
-
     full = force.shape
     species, planes, cells = full
     edge = (5, species, 2, cells)
@@ -288,8 +328,9 @@
     above = lax.ppermute(low, "space", down)
     nodes = (count,) + full
     params = (mixing, diffusivity, velocity)
+    shapes = [param.shape for param in params]
     fields = (start, before, force, force_before, decay_rate)
-    v1, handed = call(inner_kernel, [nodes, full], "vvvvvsss", [nodes, nodes], 2**25)(
+    v1, handed = call(inner_kernel, [nodes, full], "vvvvvhhh", [nodes, nodes], 2**25, shapes)(
         *fields, *params
     )
     small = (species, 8, cells)
@@ -297,10 +338,11 @@
     (out,) = call(
         outer_kernel,
         [(1, 1) + full],
-        "ss" + "v" * 10 + "sss",
+        "s" + "v" * 10 + "hhh",
         [(5,) + small, edges, edges, edges, small, nodes],
         2**25,
-    )(where_am_i, own_row, *fields, initial, below, above, v1, handed, *params)
+        shapes,
+    )(where_am_i, *fields, initial, below, above, v1, handed, *params)
     return out
 
 

time: 60.2 us -> 56.5 us (0.939)
  the two profiles are of different devices: /device:TPU:188 before, /device:TPU:387 now
where the time goes in v3:
time: 56.5 us; the launch traced here: 56.2 us
  blocking collectives  20.3 us (36%)
  starting transfers between devices  18.7 us (33%)
  Pallas kernels  8.81 us (16%)
  waiting for transfers between devices  7.15 us (13%)
  local copies, waits for them, and re-layouts  0.77 us (1%)
    all_gather x1, blocking collectives, team_base(): lax.all_gather(state, 'tm', axis=0, tiled=True, axis_index_groups=groups)  11.4 us
    all_gather x1, blocking collectives, team_base(): gathered = lax.all_gather(force, 'tm', axis_index_groups=groups)  8.89 us
    ppermute x7, starting transfers between devices, send(): return lax.ppermute(value, 'tm', pairs)  8.18 us
    ppermute x7, waiting for transfers between devices, send(): return lax.ppermute(value, 'tm', pairs)  7.14 us
    ppermute x1, starting transfers between devices, body(): above = lax.ppermute(low, 'space', down)  6.76 us
    pallas_call x1, Pallas kernels, body(): call(outer_kernel, [(1, 1) + full], 's' + 'v' * 10 + 'hhh', [(5,) + small...  4.48 us
    pallas_call x1, Pallas kernels, body(): call(inner_kernel, [nodes, full], 'vvvvvhhh', [nodes, nodes], 2 ** 25, sh...  3.65 us
    ppermute x1, starting transfers between devices, body(): below = lax.ppermute(high, 'space', up)  3.12 us
  transfers between devices with their start and end apart: 10, of which 3 were waited for; matrix products, arithmetic and copies ran while one was open for 0% of the time, Pallas kernels for 6%

profile of v3, /device:TPU:387, one launch (start us, length us, event | category | flops | bytes accessed | tf_op | source)
XLA Modules:
  0.0 56.2 jit_solution(14911091898804582018)
XLA Ops:
  0.0 0.0 copy-start
  0.0 0.0 copy-start.2
  0.0 8.9 %all_gather.6.gathered_ref = f32[4,8,16,256]{3,2,1,0:T(8,128)S(1)} all-gather(f32[1,8,16,256]{3,2,1,0:T(8,128)} %param.7), channel_id=1, replica_groups={{0,32,64,96},{128,160,192,224},{256,288,320,352},{384,416,448,480},{512..., dimensions={0}, use_global_device_ids=true | all-gather | bytes 655360 | tf_op jit(solution)/shard_map/all_gather | solution.py:273
  8.9 0.0 copy-done
  8.9 0.0 copy-done.2
  8.9 0.7 %collective-permute-start = (f32[2,16,256]{2,1,0:T(8,128)S(1)}, f32[2,16,256]{2,1,0:T(8,128)S(1)}, u32[]{:S(2)}, u32[]{:S(2)}) collective-permute-start(f32[2,16,256]{2,1,0:T(8,128)S(1)} %get-tuple-element.23), channel_id=1, source_target_pairs={{0,128},{32,160},{64,192},{96,224},{1,129},{33,161},{65,193},{97,2... | collective-permute-start | bytes 98312 | tf_op jit(solution)/shard_map/ppermute | solution.py:289
  9.6 0.0 collective-permute-done
  9.7 0.7 %collective-permute-start.1 = (f32[2,16,256]{2,1,0:T(8,128)S(1)}, f32[2,16,256]{2,1,0:T(8,128)S(1)}, u32[]{:S(2)}, u32[]{:S(2)}) collective-permute-start(f32[2,16,256]{2,1,0:T(8,128)S(1)} %get-tuple-element.21), channel_id=1, source_target_pairs={{128,256},{160,288},{192,320},{224,352},{129,257},{161,289},{193,3... | collective-permute-start | bytes 98312 | tf_op jit(solution)/shard_map/ppermute | solution.py:289
  10.3 0.0 collective-permute-done.1
  10.4 1.3 %collective-permute-start.2 = (f32[2,16,256]{2,1,0:T(8,128)S(1)}, f32[2,16,256]{2,1,0:T(8,128)S(1)}, u32[]{:S(2)}, u32[]{:S(2)}) collective-permute-start(f32[2,16,256]{2,1,0:T(8,128)S(1)} %multiply_add_fusion.3), channel_id=1, source_target_pairs={{256,384},{288,416},{320,448},{352,480},{257,385},{289,417},{321,4... | collective-permute-start | bytes 98312 | tf_op jit(solution)/shard_map/ppermute | solution.py:289
  11.7 0.7 %collective-permute-start.4 = (f32[2,16,256]{2,1,0:T(8,128)S(1)}, f32[2,16,256]{2,1,0:T(8,128)S(1)}, u32[]{:S(2)}, u32[]{:S(2)}) collective-permute-start(f32[2,16,256]{2,1,0:T(8,128)S(1)} %get-tuple-element.24), channel_id=1, source_target_pairs={{512,640},{544,672},{576,704},{608,736},{768,896},{800,928},{832,9... | collective-permute-start | bytes 98312 | tf_op jit(solution)/shard_map/ppermute | solution.py:289
  12.4 5.1 %collective-permute-done.2 = f32[2,16,256]{2,1,0:T(8,128)S(1)} collective-permute-done((f32[2,16,256]{2,1,0:T(8,128)S(1)}, f32[2,16,256]{2,1,0:T(8,128)S(1)}, u32[]{:S(2)}, u32[]{:S(2)}) %collective-permute-start.2) | collective-permute-done | bytes 32800 | tf_op jit(solution)/shard_map/ppermute | solution.py:289
  17.5 2.8 %collective-permute-start.3 = (f32[2,16,256]{2,1,0:T(8,128)S(1)}, f32[2,16,256]{2,1,0:T(8,128)S(1)}, u32[]{:S(2)}, u32[]{:S(2)}) collective-permute-start(f32[2,16,256]{2,1,0:T(8,128)S(1)} %get-tuple-element.19), channel_id=1, source_target_pairs={{384,640},{416,672},{448,704},{480,736},{385,641},{417,673},{449,7... | collective-permute-start | bytes 98312 | tf_op jit(solution)/shard_map/ppermute | solution.py:289
  20.4 0.0 collective-permute-done.4
  20.4 1.0 %collective-permute-done.3 = f32[2,16,256]{2,1,0:T(8,128)S(1)} collective-permute-done((f32[2,16,256]{2,1,0:T(8,128)S(1)}, f32[2,16,256]{2,1,0:T(8,128)S(1)}, u32[]{:S(2)}, u32[]{:S(2)}) %collective-permute-start.3) | collective-permute-done | bytes 32800 | tf_op jit(solution)/shard_map/ppermute | solution.py:289
  21.4 0.0 copy-start.1
  21.4 1.4 %collective-permute-start.5 = (f32[2,16,256]{2,1,0:T(8,128)S(1)}, f32[2,16,256]{2,1,0:T(8,128)S(1)}, u32[]{:S(2)}, u32[]{:S(2)}) collective-permute-start(f32[2,16,256]{2,1,0:T(8,128)S(1)} %multiply_add_fusion.1), channel_id=1, source_target_pairs={{384,512},{416,544},{448,576},{480,608},{640,896},{672,928},{704,9... | collective-permute-start | bytes 98312 | tf_op jit(solution)/shard_map/ppermute | solution.py:289
  22.8 1.0 %collective-permute-done.5 = f32[2,16,256]{2,1,0:T(8,128)S(1)} collective-permute-done((f32[2,16,256]{2,1,0:T(8,128)S(1)}, f32[2,16,256]{2,1,0:T(8,128)S(1)}, u32[]{:S(2)}, u32[]{:S(2)}) %collective-permute-start.5) | collective-permute-done | bytes 32800 | tf_op jit(solution)/shard_map/ppermute | solution.py:289
  23.9 0.7 %collective-permute-start.6 = (f32[2,16,256]{2,1,0:T(8,128)S(1)}, f32[2,16,256]{2,1,0:T(8,128)S(1)}, u32[]{:S(2)}, u32[]{:S(2)}) collective-permute-start(f32[2,16,256]{2,1,0:T(8,128)S(1)} %multiply_add_fusion), channel_id=1, source_target_pairs={{640,768},{672,800},{704,832},{736,864},{641,769},{673,801},{705,8... | collective-permute-start | bytes 98312 | tf_op jit(solution)/shard_map/ppermute | solution.py:289
  24.5 0.0 copy-done.1
  24.6 0.7 %collective-permute-start.7 = (f32[8,16,256]{2,1,0:T(8,128)S(1)}, f32[8,16,256]{2,1,0:T(8,128)S(1)}, u32[]{:S(2)}, u32[]{:S(2)}) collective-permute-start(f32[8,16,256]{2,1,0:T(8,128)S(1)} %bitcast.37), channel_id=1, source_target_pairs={{96,128},{224,256},{352,384},{480,512},{608,640},{736,768},{864,89... | collective-permute-start | bytes 393224 | tf_op jit(solution)/shard_map/ppermute | solution.py:272
  25.2 0.1 stack.19.place_ref
  25.3 0.0 collective-permute-done.6
  25.4 11.4 %all_gather.7.base_ref = f32[8,16,256]{2,1,0:T(8,128)S(1)} all-gather(f32[2,16,256]{2,1,0:T(8,128)S(1)} %select_select_fusion), channel_id=1, replica_groups={{0,32,64,96},{128,160,192,224},{256,288,320,352},{384,416,448,480},{512..., dimensions={0}, use_global_device_ids=true | all-gather | bytes 163840 | tf_op jit(solution)/shard_map/all_gather | solution.py:306
  36.8 0.0 collective-permute-done.7.handover_ref
  36.8 0.7 %shard_map.64 = (f32[8,16,256]{2,1,0:T(8,128)S(1)}, f32[8,16,256]{2,1,0:T(8,128)S(1)}, f32[8,16,256]{2,1,0:T(8,128)S(1)}, f32[5,8,2,256]{3,2,1,0:T(2,128)S(1)}, f32[5,8,2,256]{3,2,1,0:T(2,128)S(1)}) custom-call(s32[5]{0:T(128)S(1)} %stack.19.place_ref, f32[8,16,256]{2,1,0:T(8,128)S(1)} %all_gather.7.base_ref, f32[4,8,16,256]{3,2,1,0:T(8,128)S(1)} %all_gather.6.gathered_ref, ...), custom_call_target="tpu_custom_call" | custom-call | flops 1048576 | bytes 131072 | tf_op jit(solution)/shard_map/pallas_call | solution.py:322
  37.4 0.0 copy-start.3
  37.4 3.1 %collective-permute-start.8 = (f32[5,8,2,256]{3,2,1,0:T(2,128)S(1)}, f32[5,8,2,256]{3,2,1,0:T(2,128)S(1)}, u32[]{:S(2)}, u32[]{:S(2)}) collective-permute-start(f32[5,8,2,256]{3,2,1,0:T(2,128)S(1)} %get-tuple-element.15), channel_id=1, source_target_pairs={{0,8},{8,16},{16,24},{1,9},{9,17},{17,25},{2,10},{10,18},{18,26},{... | collective-permute-start | bytes 245768 | tf_op jit(solution)/shard_map/ppermute | solution.py:327
  40.6 6.8 %collective-permute-start.9 = (f32[5,8,2,256]{3,2,1,0:T(2,128)S(1)}, f32[5,8,2,256]{3,2,1,0:T(2,128)S(1)}, u32[]{:S(2)}, u32[]{:S(2)}) collective-permute-start(f32[5,8,2,256]{3,2,1,0:T(2,128)S(1)} %get-tuple-element.16), channel_id=1, source_target_pairs={{8,0},{16,8},{24,16},{9,1},{17,9},{25,17},{10,2},{18,10},{26,18},{... | collective-permute-start | bytes 245768 | tf_op jit(solution)/shard_map/ppermute | solution.py:328
  47.3 0.0 copy-start.4
  47.4 0.0 copy-start.5
  47.4 0.0 copy-done.3
  47.4 0.7 %copy-done.4 = f32[3,8]{1,0:T(4,128)S(1)} copy-done((f32[3,8]{1,0:T(4,128)S(1)}, f32[3,8]{1,0:T(4,128)}, u32[]{:S(2)}) %copy-start.4) | copy-done | bytes 120
  48.0 0.0 copy-done.5
  48.0 3.6 %shard_map.65 = (f32[8,8,16,256]{3,2,1,0:T(8,128)S(1)}, f32[8,16,256]{2,1,0:T(8,128)S(1)}) custom-call(f32[8,16,256]{2,1,0:T(8,128)S(1)} %get-tuple-element.12.start_ref, f32[8,16,256]{2,1,0:T(8,128)S(1)} %get-tuple-element.13.before_ref, f32[8,16,256]{2,1,0:T(8,128)S(1)} %bitcast.39, f32[8,16,256]{2,1,0:T(8,128)S(1)} %get-tuple-element.14.force_before_ref, ...), custom_call_target="tpu_custom_call" | custom-call | flops 33554432 | bytes 4194304 | tf_op jit(solution)/shard_map/pallas_call | solution.py:333
  51.7 0.0 collective-permute-done.8.below_ref
  51.7 0.0 collective-permute-done.9.above_ref
  51.7 4.5 %shard_map.66 = f32[1,1,8,16,256]{4,3,2,1,0:T(8,128)} custom-call(s32[5]{0:T(128)S(1)} %stack.19.place_ref, f32[8,16,256]{2,1,0:T(8,128)S(1)} %get-tuple-element.12.start_ref, f32[8,16,256]{2,1,0:T(8,128)S(1)} %get-tuple-element.13.before_ref, f32[8,16,256]{2,1,0:T(8,128)S(1)} %bitcast.40, f32[8,16,256]{2,1,0:T(8,128)S(1)} %get-tuple-element.14.force_before_ref, ...), custom_call_target="tpu_custom_call" | custom-call | flops 33554432 | bytes 4194304 | tf_op jit(solution)/shard_map/pallas_call | solution.py:338
  (7 shorter events, 0.2 us)
Async XLA Ops:
  0.0 8.9 %copy-start = (f32[8,16,256]{2,1,0:T(8,128)S(1)}, f32[8,16,256]{2,1,0:T(8,128)}, u32[]{:S(2)}) copy-start(f32[8,16,256]{2,1,0:T(8,128)} %decay_ref.5) | copy-start | bytes 393220
  0.0 8.9 %copy-start.2 = (f32[8,16,256]{2,1,0:T(8,128)S(1)}, f32[8,16,256]{2,1,0:T(8,128)}, u32[]{:S(2)}) copy-start(f32[8,16,256]{2,1,0:T(8,128)} %initial_ref.1) | copy-start | bytes 393220
  8.9 0.7 %collective-permute-start = (f32[2,16,256]{2,1,0:T(8,128)S(1)}, f32[2,16,256]{2,1,0:T(8,128)S(1)}, u32[]{:S(2)}, u32[]{:S(2)}) collective-permute-start(f32[2,16,256]{2,1,0:T(8,128)S(1)} %get-tuple-element.23), channel_id=1, source_target_pairs={{0,128},{32,160},{64,192},{96,224},{1,129},{33,161},{65,193},{97,2... | collective-permute-start | bytes 98312 | tf_op jit(solution)/shard_map/ppermute | solution.py:289
  9.7 0.7 %collective-permute-start.1 = (f32[2,16,256]{2,1,0:T(8,128)S(1)}, f32[2,16,256]{2,1,0:T(8,128)S(1)}, u32[]{:S(2)}, u32[]{:S(2)}) collective-permute-start(f32[2,16,256]{2,1,0:T(8,128)S(1)} %get-tuple-element.21), channel_id=1, source_target_pairs={{128,256},{160,288},{192,320},{224,352},{129,257},{161,289},{193,3... | collective-permute-start | bytes 98312 | tf_op jit(solution)/shard_map/ppermute | solution.py:289
  10.4 7.1 %collective-permute-start.2 = (f32[2,16,256]{2,1,0:T(8,128)S(1)}, f32[2,16,256]{2,1,0:T(8,128)S(1)}, u32[]{:S(2)}, u32[]{:S(2)}) collective-permute-start(f32[2,16,256]{2,1,0:T(8,128)S(1)} %multiply_add_fusion.3), channel_id=1, source_target_pairs={{256,384},{288,416},{320,448},{352,480},{257,385},{289,417},{321,4... | collective-permute-start | bytes 98312 | tf_op jit(solution)/shard_map/ppermute | solution.py:289
  11.7 8.7 %collective-permute-start.4 = (f32[2,16,256]{2,1,0:T(8,128)S(1)}, f32[2,16,256]{2,1,0:T(8,128)S(1)}, u32[]{:S(2)}, u32[]{:S(2)}) collective-permute-start(f32[2,16,256]{2,1,0:T(8,128)S(1)} %get-tuple-element.24), channel_id=1, source_target_pairs={{512,640},{544,672},{576,704},{608,736},{768,896},{800,928},{832,9... | collective-permute-start | bytes 98312 | tf_op jit(solution)/shard_map/ppermute | solution.py:289
  17.5 3.8 %collective-permute-start.3 = (f32[2,16,256]{2,1,0:T(8,128)S(1)}, f32[2,16,256]{2,1,0:T(8,128)S(1)}, u32[]{:S(2)}, u32[]{:S(2)}) collective-permute-start(f32[2,16,256]{2,1,0:T(8,128)S(1)} %get-tuple-element.19), channel_id=1, source_target_pairs={{384,640},{416,672},{448,704},{480,736},{385,641},{417,673},{449,7... | collective-permute-start | bytes 98312 | tf_op jit(solution)/shard_map/ppermute | solution.py:289
  21.4 3.2 %copy-start.1 = (f32[1,8,16,256]{3,2,1,0:T(8,128)S(1)}, f32[1,8,16,256]{3,2,1,0:T(8,128)}, u32[]{:S(2)}) copy-start(f32[1,8,16,256]{3,2,1,0:T(8,128)} %param.7) | copy-start | bytes 393220
  21.4 2.4 %collective-permute-start.5 = (f32[2,16,256]{2,1,0:T(8,128)S(1)}, f32[2,16,256]{2,1,0:T(8,128)S(1)}, u32[]{:S(2)}, u32[]{:S(2)}) collective-permute-start(f32[2,16,256]{2,1,0:T(8,128)S(1)} %multiply_add_fusion.1), channel_id=1, source_target_pairs={{384,512},{416,544},{448,576},{480,608},{640,896},{672,928},{704,9... | collective-permute-start | bytes 98312 | tf_op jit(solution)/shard_map/ppermute | solution.py:289
  23.9 1.5 %collective-permute-start.6 = (f32[2,16,256]{2,1,0:T(8,128)S(1)}, f32[2,16,256]{2,1,0:T(8,128)S(1)}, u32[]{:S(2)}, u32[]{:S(2)}) collective-permute-start(f32[2,16,256]{2,1,0:T(8,128)S(1)} %multiply_add_fusion), channel_id=1, source_target_pairs={{640,768},{672,800},{704,832},{736,864},{641,769},{673,801},{705,8... | collective-permute-start | bytes 98312 | tf_op jit(solution)/shard_map/ppermute | solution.py:289
  24.6 12.2 %collective-permute-start.7 = (f32[8,16,256]{2,1,0:T(8,128)S(1)}, f32[8,16,256]{2,1,0:T(8,128)S(1)}, u32[]{:S(2)}, u32[]{:S(2)}) collective-permute-start(f32[8,16,256]{2,1,0:T(8,128)S(1)} %bitcast.37), channel_id=1, source_target_pairs={{96,128},{224,256},{352,384},{480,512},{608,640},{736,768},{864,89... | collective-permute-start | bytes 393224 | tf_op jit(solution)/shard_map/ppermute | solution.py:272
  37.4 9.9 %copy-start.3 = (f32[8,8]{1,0:T(8,128)S(1)}, f32[8,8]{1,0:T(8,128)}, u32[]{:S(2)}) copy-start(f32[8,8]{1,0:T(8,128)} %mix_hbm.3) | copy-start | bytes 772
  37.4 14.2 %collective-permute-start.8 = (f32[5,8,2,256]{3,2,1,0:T(2,128)S(1)}, f32[5,8,2,256]{3,2,1,0:T(2,128)S(1)}, u32[]{:S(2)}, u32[]{:S(2)}) collective-permute-start(f32[5,8,2,256]{3,2,1,0:T(2,128)S(1)} %get-tuple-element.15), channel_id=1, source_target_pairs={{0,8},{8,16},{16,24},{1,9},{9,17},{17,25},{2,10},{10,18},{18,26},{... | collective-permute-start | bytes 245768 | tf_op jit(solution)/shard_map/ppermute | solution.py:327
  40.6 11.1 %collective-permute-start.9 = (f32[5,8,2,256]{3,2,1,0:T(2,128)S(1)}, f32[5,8,2,256]{3,2,1,0:T(2,128)S(1)}, u32[]{:S(2)}, u32[]{:S(2)}) collective-permute-start(f32[5,8,2,256]{3,2,1,0:T(2,128)S(1)} %get-tuple-element.16), channel_id=1, source_target_pairs={{8,0},{16,8},{24,16},{9,1},{17,9},{25,17},{10,2},{18,10},{26,18},{... | collective-permute-start | bytes 245768 | tf_op jit(solution)/shard_map/ppermute | solution.py:328
  47.3 0.7 %copy-start.4 = (f32[3,8]{1,0:T(4,128)S(1)}, f32[3,8]{1,0:T(4,128)}, u32[]{:S(2)}) copy-start(f32[3,8]{1,0:T(4,128)} %vel_hbm.3) | copy-start | bytes 292
  47.4 0.7 %copy-start.5 = (f32[8]{0:T(128)S(1)}, f32[8]{0:T(128)}, u32[]{:S(2)}) copy-start(f32[8]{0:T(128)} %diff_hbm.3) | copy-start | bytes 100

commit v4 on v3

--- a/solution.py
+++ b/solution.py
@@ -157,8 +157,9 @@
                 vel_ref, v_ref, w_ref, v1_ref, handed_ref, ready)
 
 
-def start_kernel(place_ref, base_ref, gathered_ref, handover_ref, force_ref, decay_ref, start_ref,
-                 before_ref, force_before_ref, low_ref, high_ref):
+def start_kernel(place_ref, base_ref, gathered_ref, handover_ref, force_ref, decay_ref, mix_hbm, diff_hbm,
+                 vel_hbm, start_ref, before_ref, force_before_ref, low_ref, high_ref):
+    del mix_hbm, diff_hbm, vel_hbm
     member = place_ref[0]
     planes = base_ref.shape[1]
     for s in range(base_ref.shape[0]):
@@ -248,7 +249,7 @@
 def call(kernel, outs, ins, scratch, cost, params=()):
     spaces = [{"s": pltpu.SMEM, "v": pltpu.VMEM, "h": pltpu.HBM}[kind] for kind in ins]
     scratch = [pltpu.VMEM(shape, jnp.float32) for shape in scratch]
-    if "h" in ins:
+    if params:
         scratch += [pltpu.SMEM(shape, jnp.float32) for shape in params]
         scratch += [pltpu.SemaphoreType.DMA((len(params),))]
     return pl.pallas_call(
@@ -294,15 +295,16 @@
     for g in range(middle):
         arrived = send(factor4 * state + summed, (g, g + 1))
         state = jnp.where(team == g + 1, arrived, state)
-    waiting = []
-    for g in range(middle, teams, 2):
-        routes = waiting + ([(g, g + 2)] if g + 2 < teams else [])
-        if routes:
-            arrived = send(factor4 * state + summed, *routes)
-            for _, t in waiting:
-                state = jnp.where(team == t, arrived, state)
+    anchor = 0.0 * handover[0, :1, :1]
+    beside = []
+    for g in range(middle, teams - 1, 2):
+        ahead = factor4 * state + summed + anchor
+        if g + 2 < teams:
+            arrived = send(ahead, (g, g + 2))
             state = jnp.where(team == g + 2, factor4 * arrived + near, state)
-        waiting = [(g, g + 1)] if g + 1 < teams else []
+        beside.append((g + 1, send(ahead, (g, g + 1))))
+    for t, arrived in beside:
+        state = jnp.where(team == t, arrived, state)
     base = lax.all_gather(state, "tm", axis=0, tiled=True, axis_index_groups=groups)
     return base, gathered, handover
 
@@ -317,17 +319,17 @@
     base, gathered, handover = team_base(initial, force, decay_rate)
     where_am_i = jnp.stack([place % TEAM, node, place, tile, jnp.int32(tiles)]).astype(jnp.int32)
     full = force.shape
+    params = (mixing, diffusivity, velocity)
     species, planes, cells = full
     edge = (5, species, 2, cells)
     start, before, force_before, low, high = call(
-        start_kernel, [full, full, full, edge, edge], "svvvvv", [], 2**20
-    )(where_am_i, base, gathered, handover, force, decay_rate)
+        start_kernel, [full, full, full, edge, edge], "svvvvvhhh", [], 2**20
+    )(where_am_i, base, gathered, handover, force, decay_rate, *params)
     up = [(i, i + 1) for i in range(tiles - 1)]
     down = [(j, i) for i, j in up]
     below = lax.ppermute(high, "space", up)
     above = lax.ppermute(low, "space", down)
     nodes = (count,) + full
-    params = (mixing, diffusivity, velocity)
     shapes = [param.shape for param in params]
     fields = (start, before, force, force_before, decay_rate)
     v1, handed = call(inner_kernel, [nodes, full], "vvvvvhhh", [nodes, nodes], 2**25, shapes)(

time: 56.5 us -> 53.4 us (0.945)
  the two profiles are of different devices: /device:TPU:387 before, /device:TPU:826 now
where the time goes in v4:
time: 53.4 us; the launch traced here: 53.1 us
  starting transfers between devices  16.8 us (31%)
  blocking collectives  12.9 us (24%)
  waiting for transfers between devices  12.8 us (24%)
  Pallas kernels  8.79 us (16%)
  between operations  0.91 us (2%)
  local copies, waits for them, and re-layouts  0.66 us (1%)
    ppermute x8, waiting for transfers between devices, send(): return lax.ppermute(value, 'tm', pairs)  11.4 us
    ppermute x8, starting transfers between devices, send(): return lax.ppermute(value, 'tm', pairs)  9.69 us
    all_gather x1, blocking collectives, team_base(): gathered = lax.all_gather(force, 'tm', axis_index_groups=groups)  7.48 us
    all_gather x1, blocking collectives, team_base(): lax.all_gather(state, 'tm', axis=0, tiled=True, axis_index_groups=groups)  5.43 us
    pallas_call x1, Pallas kernels, body(): call(outer_kernel, [(1, 1) + full], 's' + 'v' * 10 + 'hhh', [(5,) + small...  4.47 us
    pallas_call x1, Pallas kernels, body(): call(inner_kernel, [nodes, full], 'vvvvvhhh', [nodes, nodes], 2 ** 25, sh...  3.64 us
    ppermute x1, starting transfers between devices, body(): below = lax.ppermute(high, 'space', up)  3.4 us
    ppermute x1, starting transfers between devices, body(): above = lax.ppermute(low, 'space', down)  2.44 us
  transfers between devices with their start and end apart: 11, of which 3 were waited for; matrix products, arithmetic and copies ran while one was open for 1% of the time, Pallas kernels for 7%

profile of v4, /device:TPU:826, one launch (start us, length us, event | category | flops | bytes accessed | tf_op | source)
XLA Modules:
  0.0 53.1 jit_solution(13603367710768331942)
XLA Ops:
  0.0 0.0 copy-start
  0.0 0.0 copy-start.2
  0.0 7.5 %all_gather.6.gathered_ref = f32[4,8,16,256]{3,2,1,0:T(8,128)S(1)} all-gather(f32[1,8,16,256]{3,2,1,0:T(8,128)} %param.7), channel_id=1, replica_groups={{0,32,64,96},{128,160,192,224},{256,288,320,352},{384,416,448,480},{512..., dimensions={0}, use_global_device_ids=true | all-gather | bytes 655360 | tf_op jit(solution)/shard_map/all_gather | solution.py:274
  7.5 0.0 copy-done
  7.5 0.0 copy-done.2
  7.5 0.0 copy-start.1
  7.5 0.8 %collective-permute-start = (f32[2,16,256]{2,1,0:T(8,128)S(1)}, f32[2,16,256]{2,1,0:T(8,128)S(1)}, u32[]{:S(2)}, u32[]{:S(2)}) collective-permute-start(f32[2,16,256]{2,1,0:T(8,128)S(1)} %get-tuple-element.23), channel_id=1, source_target_pairs={{0,128},{32,160},{64,192},{96,224},{1,129},{33,161},{65,193},{97,2... | collective-permute-start | bytes 98312 | tf_op jit(solution)/shard_map/ppermute | solution.py:290
  8.4 0.0 collective-permute-done
  8.4 0.7 %collective-permute-start.1 = (f32[2,16,256]{2,1,0:T(8,128)S(1)}, f32[2,16,256]{2,1,0:T(8,128)S(1)}, u32[]{:S(2)}, u32[]{:S(2)}) collective-permute-start(f32[2,16,256]{2,1,0:T(8,128)S(1)} %get-tuple-element.21), channel_id=1, source_target_pairs={{128,256},{160,288},{192,320},{224,352},{129,257},{161,289},{193,3... | collective-permute-start | bytes 98312 | tf_op jit(solution)/shard_map/ppermute | solution.py:290
  9.1 0.0 copy-done.1
  9.1 1.3 %collective-permute-start.3 = (f32[8,16,256]{2,1,0:T(8,128)S(1)}, f32[8,16,256]{2,1,0:T(8,128)S(1)}, u32[]{:S(2)}, u32[]{:S(2)}) collective-permute-start(f32[8,16,256]{2,1,0:T(8,128)S(1)} %bitcast.38), channel_id=1, source_target_pairs={{96,128},{224,256},{352,384},{480,512},{608,640},{736,768},{864,89... | collective-permute-start | bytes 393224 | tf_op jit(solution)/shard_map/ppermute | solution.py:273
  10.4 0.0 collective-permute-done.1
  10.4 0.7 %collective-permute-start.2 = (f32[2,16,256]{2,1,0:T(8,128)S(1)}, f32[2,16,256]{2,1,0:T(8,128)S(1)}, u32[]{:S(2)}, u32[]{:S(2)}) collective-permute-start(f32[2,16,256]{2,1,0:T(8,128)S(1)} %multiply_add_fusion), channel_id=1, source_target_pairs={{256,384},{288,416},{320,448},{352,480},{257,385},{289,417},{321,4... | collective-permute-start | bytes 98312 | tf_op jit(solution)/shard_map/ppermute | solution.py:290
  11.1 4.3 %collective-permute-start.5 = (f32[2,16,256]{2,1,0:T(8,128)S(1)}, f32[2,16,256]{2,1,0:T(8,128)S(1)}, u32[]{:S(2)}, u32[]{:S(2)}) collective-permute-start(f32[2,16,256]{2,1,0:T(8,128)S(1)} %get-tuple-element.24), channel_id=1, source_target_pairs={{512,640},{544,672},{576,704},{608,736},{768,896},{800,928},{832,9... | collective-permute-start | bytes 98312 | tf_op jit(solution)/shard_map/ppermute | solution.py:290
  15.4 1.2 %collective-permute-done.3.handover_ref = f32[8,16,256]{2,1,0:T(8,128)S(1)} collective-permute-done((f32[8,16,256]{2,1,0:T(8,128)S(1)}, f32[8,16,256]{2,1,0:T(8,128)S(1)}, u32[]{:S(2)}, u32[]{:S(2)}) %collective-permute-start.3) | collective-permute-done | bytes 131104 | tf_op jit(solution)/shard_map/ppermute | solution.py:273
  16.6 0.5 %slice.20 = f32[1,1,1]{2,1,0:T(1,128)} slice(f32[8,16,256]{2,1,0:T(8,128)S(1)} %collective-permute-done.3.handover_ref), slice={[0:1], [0:1], [0:1]} | slice | bytes 8 | tf_op jit(solution)/shard_map/slice | solution.py:298
  17.8 0.0 collective-permute-done.2
  17.8 0.7 %collective-permute-start.4 = (f32[2,16,256]{2,1,0:T(8,128)S(1)}, f32[2,16,256]{2,1,0:T(8,128)S(1)}, u32[]{:S(2)}, u32[]{:S(2)}) collective-permute-start(f32[2,16,256]{2,1,0:T(8,128)S(1)} %get-tuple-element.19), channel_id=1, source_target_pairs={{384,640},{416,672},{448,704},{480,736},{385,641},{417,673},{449,7... | collective-permute-start | bytes 98312 | tf_op jit(solution)/shard_map/ppermute | solution.py:290
  18.5 0.7 %collective-permute-start.7 = (f32[2,16,256]{2,1,0:T(8,128)S(1)}, f32[2,16,256]{2,1,0:T(8,128)S(1)}, u32[]{:S(2)}, u32[]{:S(2)}) collective-permute-start(f32[2,16,256]{2,1,0:T(8,128)S(1)} %get-tuple-element.19), channel_id=1, source_target_pairs={{384,512},{416,544},{448,576},{480,608},{385,513},{417,545},{449,5... | collective-permute-start | bytes 98312 | tf_op jit(solution)/shard_map/ppermute | solution.py:290
  19.2 0.0 collective-permute-done.5
  19.2 0.0 collective-permute-done.4
  19.2 0.7 %collective-permute-start.8 = (f32[2,16,256]{2,1,0:T(8,128)S(1)}, f32[2,16,256]{2,1,0:T(8,128)S(1)}, u32[]{:S(2)}, u32[]{:S(2)}) collective-permute-start(f32[2,16,256]{2,1,0:T(8,128)S(1)} %add_add_fusion), channel_id=1, source_target_pairs={{640,896},{672,928},{704,960},{736,992},{641,897},{673,929},{705,9... | collective-permute-start | bytes 98312 | tf_op jit(solution)/shard_map/ppermute | solution.py:290
  19.9 1.3 %collective-permute-start.6 = (f32[2,16,256]{2,1,0:T(8,128)S(1)}, f32[2,16,256]{2,1,0:T(8,128)S(1)}, u32[]{:S(2)}, u32[]{:S(2)}) collective-permute-start(f32[2,16,256]{2,1,0:T(8,128)S(1)} %add_add_fusion), channel_id=1, source_target_pairs={{640,768},{672,800},{704,832},{736,864},{641,769},{673,801},{705,8... | collective-permute-start | bytes 98312 | tf_op jit(solution)/shard_map/ppermute | solution.py:290
  21.2 0.1 stack.19.place_ref
  21.3 0.0 collective-permute-done.7
  21.3 0.0 collective-permute-done.8
  21.3 11.4 %collective-permute-done.6 = f32[2,16,256]{2,1,0:T(8,128)S(1)} collective-permute-done((f32[2,16,256]{2,1,0:T(8,128)S(1)}, f32[2,16,256]{2,1,0:T(8,128)S(1)}, u32[]{:S(2)}, u32[]{:S(2)}) %collective-permute-start.6) | collective-permute-done | bytes 32800 | tf_op jit(solution)/shard_map/ppermute | solution.py:290
  32.7 0.0 copy-start.3
  32.7 0.0 copy-start.4
  32.7 0.0 copy-start.5
  32.7 5.4 %all_gather.7.base_ref = f32[8,16,256]{2,1,0:T(8,128)S(1)} all-gather(f32[2,16,256]{2,1,0:T(8,128)S(1)} %select_select_fusion), channel_id=1, replica_groups={{0,32,64,96},{128,160,192,224},{256,288,320,352},{384,416,448,480},{512..., dimensions={0}, use_global_device_ids=true | all-gather | bytes 163840 | tf_op jit(solution)/shard_map/all_gather | solution.py:308
  38.2 0.0 copy-done.3
  38.2 0.0 copy-done.4
  38.2 0.0 copy-done.5
  38.2 0.7 %shard_map.64 = (f32[8,16,256]{2,1,0:T(8,128)S(1)}, f32[8,16,256]{2,1,0:T(8,128)S(1)}, f32[8,16,256]{2,1,0:T(8,128)S(1)}, f32[5,8,2,256]{3,2,1,0:T(2,128)S(1)}, f32[5,8,2,256]{3,2,1,0:T(2,128)S(1)}) custom-call(s32[5]{0:T(128)S(1)} %stack.19.place_ref, f32[8,16,256]{2,1,0:T(8,128)S(1)} %all_gather.7.base_ref, f32[4,8,16,256]{3,2,1,0:T(8,128)S(1)} %all_gather.6.gathered_ref, ...), custom_call_target="tpu_custom_call" | custom-call | flops 1048576 | bytes 131072 | tf_op jit(solution)/shard_map/pallas_call | solution.py:325
  38.8 3.4 %collective-permute-start.9 = (f32[5,8,2,256]{3,2,1,0:T(2,128)S(1)}, f32[5,8,2,256]{3,2,1,0:T(2,128)S(1)}, u32[]{:S(2)}, u32[]{:S(2)}) collective-permute-start(f32[5,8,2,256]{3,2,1,0:T(2,128)S(1)} %get-tuple-element.15), channel_id=1, source_target_pairs={{0,8},{8,16},{16,24},{1,9},{9,17},{17,25},{2,10},{10,18},{18,26},{... | collective-permute-start | bytes 245768 | tf_op jit(solution)/shard_map/ppermute | solution.py:330
  42.3 2.4 %collective-permute-start.10 = (f32[5,8,2,256]{3,2,1,0:T(2,128)S(1)}, f32[5,8,2,256]{3,2,1,0:T(2,128)S(1)}, u32[]{:S(2)}, u32[]{:S(2)}) collective-permute-start(f32[5,8,2,256]{3,2,1,0:T(2,128)S(1)} %get-tuple-element.16), channel_id=1, source_target_pairs={{8,0},{16,8},{24,16},{9,1},{17,9},{25,17},{10,2},{18,10},{26,18},{... | collective-permute-start | bytes 245768 | tf_op jit(solution)/shard_map/ppermute | solution.py:331
  44.7 3.6 %shard_map.65 = (f32[8,8,16,256]{3,2,1,0:T(8,128)S(1)}, f32[8,16,256]{2,1,0:T(8,128)S(1)}) custom-call(f32[8,16,256]{2,1,0:T(8,128)S(1)} %get-tuple-element.12.start_ref, f32[8,16,256]{2,1,0:T(8,128)S(1)} %get-tuple-element.13.before_ref, f32[8,16,256]{2,1,0:T(8,128)S(1)} %bitcast.40, f32[8,16,256]{2,1,0:T(8,128)S(1)} %get-tuple-element.14.force_before_ref, ...), custom_call_target="tpu_custom_call" | custom-call | flops 33554432 | bytes 4194304 | tf_op jit(solution)/shard_map/pallas_call | solution.py:335
  48.4 0.0 collective-permute-done.9.below_ref
  48.4 0.2 collective-permute-done.10.above_ref
  48.6 4.5 %shard_map.66 = f32[1,1,8,16,256]{4,3,2,1,0:T(8,128)} custom-call(s32[5]{0:T(128)S(1)} %stack.19.place_ref, f32[8,16,256]{2,1,0:T(8,128)S(1)} %get-tuple-element.12.start_ref, f32[8,16,256]{2,1,0:T(8,128)S(1)} %get-tuple-element.13.before_ref, f32[8,16,256]{2,1,0:T(8,128)S(1)} %bitcast.41, f32[8,16,256]{2,1,0:T(8,128)S(1)} %get-tuple-element.14.force_before_ref, ...), custom_call_target="tpu_custom_call" | custom-call | flops 33554432 | bytes 4194304 | tf_op jit(solution)/shard_map/pallas_call | solution.py:340
  (6 shorter events, 0.2 us)
Async XLA Ops:
  0.0 7.5 %copy-start = (f32[8,16,256]{2,1,0:T(8,128)S(1)}, f32[8,16,256]{2,1,0:T(8,128)}, u32[]{:S(2)}) copy-start(f32[8,16,256]{2,1,0:T(8,128)} %decay_ref.5) | copy-start | bytes 393220
  0.0 7.5 %copy-start.2 = (f32[8,16,256]{2,1,0:T(8,128)S(1)}, f32[8,16,256]{2,1,0:T(8,128)}, u32[]{:S(2)}) copy-start(f32[8,16,256]{2,1,0:T(8,128)} %initial_ref.1) | copy-start | bytes 393220
  7.5 1.6 %copy-start.1 = (f32[1,8,16,256]{3,2,1,0:T(8,128)S(1)}, f32[1,8,16,256]{3,2,1,0:T(8,128)}, u32[]{:S(2)}) copy-start(f32[1,8,16,256]{3,2,1,0:T(8,128)} %param.7) | copy-start | bytes 393220
  7.5 0.8 %collective-permute-start = (f32[2,16,256]{2,1,0:T(8,128)S(1)}, f32[2,16,256]{2,1,0:T(8,128)S(1)}, u32[]{:S(2)}, u32[]{:S(2)}) collective-permute-start(f32[2,16,256]{2,1,0:T(8,128)S(1)} %get-tuple-element.23), channel_id=1, source_target_pairs={{0,128},{32,160},{64,192},{96,224},{1,129},{33,161},{65,193},{97,2... | collective-permute-start | bytes 98312 | tf_op jit(solution)/shard_map/ppermute | solution.py:290
  8.4 2.0 %collective-permute-start.1 = (f32[2,16,256]{2,1,0:T(8,128)S(1)}, f32[2,16,256]{2,1,0:T(8,128)S(1)}, u32[]{:S(2)}, u32[]{:S(2)}) collective-permute-start(f32[2,16,256]{2,1,0:T(8,128)S(1)} %get-tuple-element.21), channel_id=1, source_target_pairs={{128,256},{160,288},{192,320},{224,352},{129,257},{161,289},{193,3... | collective-permute-start | bytes 98312 | tf_op jit(solution)/shard_map/ppermute | solution.py:290
  9.1 7.5 %collective-permute-start.3 = (f32[8,16,256]{2,1,0:T(8,128)S(1)}, f32[8,16,256]{2,1,0:T(8,128)S(1)}, u32[]{:S(2)}, u32[]{:S(2)}) collective-permute-start(f32[8,16,256]{2,1,0:T(8,128)S(1)} %bitcast.38), channel_id=1, source_target_pairs={{96,128},{224,256},{352,384},{480,512},{608,640},{736,768},{864,89... | collective-permute-start | bytes 393224 | tf_op jit(solution)/shard_map/ppermute | solution.py:273
  10.4 7.3 %collective-permute-start.2 = (f32[2,16,256]{2,1,0:T(8,128)S(1)}, f32[2,16,256]{2,1,0:T(8,128)S(1)}, u32[]{:S(2)}, u32[]{:S(2)}) collective-permute-start(f32[2,16,256]{2,1,0:T(8,128)S(1)} %multiply_add_fusion), channel_id=1, source_target_pairs={{256,384},{288,416},{320,448},{352,480},{257,385},{289,417},{321,4... | collective-permute-start | bytes 98312 | tf_op jit(solution)/shard_map/ppermute | solution.py:290
  11.1 8.1 %collective-permute-start.5 = (f32[2,16,256]{2,1,0:T(8,128)S(1)}, f32[2,16,256]{2,1,0:T(8,128)S(1)}, u32[]{:S(2)}, u32[]{:S(2)}) collective-permute-start(f32[2,16,256]{2,1,0:T(8,128)S(1)} %get-tuple-element.24), channel_id=1, source_target_pairs={{512,640},{544,672},{576,704},{608,736},{768,896},{800,928},{832,9... | collective-permute-start | bytes 98312 | tf_op jit(solution)/shard_map/ppermute | solution.py:290
  17.8 1.4 %collective-permute-start.4 = (f32[2,16,256]{2,1,0:T(8,128)S(1)}, f32[2,16,256]{2,1,0:T(8,128)S(1)}, u32[]{:S(2)}, u32[]{:S(2)}) collective-permute-start(f32[2,16,256]{2,1,0:T(8,128)S(1)} %get-tuple-element.19), channel_id=1, source_target_pairs={{384,640},{416,672},{448,704},{480,736},{385,641},{417,673},{449,7... | collective-permute-start | bytes 98312 | tf_op jit(solution)/shard_map/ppermute | solution.py:290
  18.5 2.8 %collective-permute-start.7 = (f32[2,16,256]{2,1,0:T(8,128)S(1)}, f32[2,16,256]{2,1,0:T(8,128)S(1)}, u32[]{:S(2)}, u32[]{:S(2)}) collective-permute-start(f32[2,16,256]{2,1,0:T(8,128)S(1)} %get-tuple-element.19), channel_id=1, source_target_pairs={{384,512},{416,544},{448,576},{480,608},{385,513},{417,545},{449,5... | collective-permute-start | bytes 98312 | tf_op jit(solution)/shard_map/ppermute | solution.py:290
  19.2 2.1 %collective-permute-start.8 = (f32[2,16,256]{2,1,0:T(8,128)S(1)}, f32[2,16,256]{2,1,0:T(8,128)S(1)}, u32[]{:S(2)}, u32[]{:S(2)}) collective-permute-start(f32[2,16,256]{2,1,0:T(8,128)S(1)} %add_add_fusion), channel_id=1, source_target_pairs={{640,896},{672,928},{704,960},{736,992},{641,897},{673,929},{705,9... | collective-permute-start | bytes 98312 | tf_op jit(solution)/shard_map/ppermute | solution.py:290
  19.9 12.8 %collective-permute-start.6 = (f32[2,16,256]{2,1,0:T(8,128)S(1)}, f32[2,16,256]{2,1,0:T(8,128)S(1)}, u32[]{:S(2)}, u32[]{:S(2)}) collective-permute-start(f32[2,16,256]{2,1,0:T(8,128)S(1)} %add_add_fusion), channel_id=1, source_target_pairs={{640,768},{672,800},{704,832},{736,864},{641,769},{673,801},{705,8... | collective-permute-start | bytes 98312 | tf_op jit(solution)/shard_map/ppermute | solution.py:290
  32.7 5.5 %copy-start.3 = (f32[8,8]{1,0:T(8,128)S(1)}, f32[8,8]{1,0:T(8,128)}, u32[]{:S(2)}) copy-start(f32[8,8]{1,0:T(8,128)} %mix_hbm.5) | copy-start | bytes 772
  32.7 5.5 %copy-start.4 = (f32[3,8]{1,0:T(4,128)S(1)}, f32[3,8]{1,0:T(4,128)}, u32[]{:S(2)}) copy-start(f32[3,8]{1,0:T(4,128)} %vel_hbm.5) | copy-start | bytes 292
  32.7 5.4 %copy-start.5 = (f32[8]{0:T(128)S(1)}, f32[8]{0:T(128)}, u32[]{:S(2)}) copy-start(f32[8]{0:T(128)} %diff_hbm.5) | copy-start | bytes 100
  38.8 9.5 %collective-permute-start.9 = (f32[5,8,2,256]{3,2,1,0:T(2,128)S(1)}, f32[5,8,2,256]{3,2,1,0:T(2,128)S(1)}, u32[]{:S(2)}, u32[]{:S(2)}) collective-permute-start(f32[5,8,2,256]{3,2,1,0:T(2,128)S(1)} %get-tuple-element.15), channel_id=1, source_target_pairs={{0,8},{8,16},{16,24},{1,9},{9,17},{17,25},{2,10},{10,18},{18,26},{... | collective-permute-start | bytes 245768 | tf_op jit(solution)/shard_map/ppermute | solution.py:330
  42.3 6.3 %collective-permute-start.10 = (f32[5,8,2,256]{3,2,1,0:T(2,128)S(1)}, f32[5,8,2,256]{3,2,1,0:T(2,128)S(1)}, u32[]{:S(2)}, u32[]{:S(2)}) collective-permute-start(f32[5,8,2,256]{3,2,1,0:T(2,128)S(1)} %get-tuple-element.16), channel_id=1, source_target_pairs={{8,0},{16,8},{24,16},{9,1},{17,9},{25,17},{10,2},{18,10},{26,18},{... | collective-permute-start | bytes 245768 | tf_op jit(solution)/shard_map/ppermute | solution.py:331

commit v5 on v4

--- a/solution.py
+++ b/solution.py
@@ -178,9 +178,12 @@
         start_ref[s] = start
         before_ref[s] = before
         force_before_ref[s] = force_before
-        for k, field in enumerate((start, before, force_ref[s], force_before, decay)):
+        for k, field in enumerate((start, force_ref[s], decay)):
             low_ref[k, s] = field[:2]
             high_ref[k, s] = field[planes - 2 :]
+        for k, field in enumerate((before, force_before)):
+            low_ref[3, s, k : k + 1] = field[:1]
+            high_ref[3, s, k : k + 1] = field[planes - 1 :]
 
 
 def outer_kernel(place_ref, start_ref, before_ref, force_ref, force_before_ref, decay_ref,
@@ -191,13 +194,18 @@
     node, slot, tile, tiles = place_ref[1], place_ref[2], place_ref[3], place_ref[4]
     species, planes, cells = start_ref.shape
     count = v_ref.shape[0]
-    for k, ref in enumerate((start_ref, before_ref, force_ref, force_before_ref, decay_ref)):
+    for k, ref in enumerate((start_ref, force_ref, decay_ref, before_ref, force_before_ref)):
         for s in range(species):
-            e_ref[k, s, 0:2] = below_ref[k, s]
+            if k < 3:
+                e_ref[k, s, 0:2] = below_ref[k, s]
+                e_ref[k, s, 6:8] = above_ref[k, s]
+            else:
+                for at in (0, 1):
+                    e_ref[k, s, at : at + 1] = below_ref[3, s, k - 3 : k - 2]
+                    e_ref[k, s, at + 6 : at + 7] = above_ref[3, s, k - 3 : k - 2]
             e_ref[k, s, 2:4] = ref[s, 0:2]
             e_ref[k, s, 4:6] = ref[s, planes - 2 : planes]
-            e_ref[k, s, 6:8] = above_ref[k, s]
-    first_sweep(e_ref.at[0], e_ref.at[1], e_ref.at[2], e_ref.at[3], e_ref.at[4], mix_ref, diff_ref,
+    first_sweep(e_ref.at[0], e_ref.at[3], e_ref.at[1], e_ref.at[4], e_ref.at[2], mix_ref, diff_ref,
                 vel_ref, v_ref, w_ref, v1e_ref, handede_ref, ready)
     edge = lax.broadcasted_iota(jnp.int32, (8, cells), 0)
     outside = ((tile == 0) & (edge == 1)) | ((tile == tiles - 1) & (edge == 6))
@@ -295,13 +303,14 @@
     for g in range(middle):
         arrived = send(factor4 * state + summed, (g, g + 1))
         state = jnp.where(team == g + 1, arrived, state)
-    anchor = 0.0 * handover[0, :1, :1]
     beside = []
     for g in range(middle, teams - 1, 2):
-        ahead = factor4 * state + summed + anchor
+        ahead = factor4 * state + summed
         if g + 2 < teams:
             arrived = send(ahead, (g, g + 2))
             state = jnp.where(team == g + 2, factor4 * arrived + near, state)
+        if g == middle:
+            ahead = ahead + 0.0 * handover[:share]
         beside.append((g + 1, send(ahead, (g, g + 1))))
     for t, arrived in beside:
         state = jnp.where(team == t, arrived, state)
@@ -321,7 +330,7 @@
     full = force.shape
     params = (mixing, diffusivity, velocity)
     species, planes, cells = full
-    edge = (5, species, 2, cells)
+    edge = (4, species, 2, cells)
     start, before, force_before, low, high = call(
         start_kernel, [full, full, full, edge, edge], "svvvvvhhh", [], 2**20
     )(where_am_i, base, gathered, handover, force, decay_rate, *params)

time: 53.4 us -> 53.1 us (level)
  the two profiles are of different devices: /device:TPU:826 before, /device:TPU:835 now
where the time goes in v5:
time: 53.1 us; the launch traced here: 52.8 us
  starting transfers between devices  18 us (34%)
  blocking collectives  14.9 us (28%)
  waiting for transfers between devices  10.5 us (20%)
  Pallas kernels  8.81 us (17%)
    ppermute x8, waiting for transfers between devices, send(): return lax.ppermute(value, 'tm', pairs)  10.5 us
    all_gather x1, blocking collectives, team_base(): gathered = lax.all_gather(force, 'tm', axis_index_groups=groups)  7.62 us
    all_gather x1, blocking collectives, team_base(): lax.all_gather(state, 'tm', axis=0, tiled=True, axis_index_groups=groups)  7.29 us
    ppermute x8, starting transfers between devices, send(): return lax.ppermute(value, 'tm', pairs)  6.69 us
    ppermute x1, starting transfers between devices, body(): above = lax.ppermute(low, 'space', down)  4.66 us
    pallas_call x1, Pallas kernels, body(): call(outer_kernel, [(1, 1) + full], 's' + 'v' * 10 + 'hhh', [(5,) + small...  4.48 us
    pallas_call x1, Pallas kernels, body(): call(inner_kernel, [nodes, full], 'vvvvvhhh', [nodes, nodes], 2 ** 25, sh...  3.64 us
    ppermute x1, starting transfers between devices, team_base(): lax.ppermute(force, 'tm', [(TEAM * g - 1, TEAM * g) for g in range(1, tea...  3.53 us
  transfers between devices with their start and end apart: 11, of which 1 were waited for; matrix products, arithmetic and copies ran while one was open for 0% of the time, Pallas kernels for 7%

profile of v5, /device:TPU:835, one launch (start us, length us, event | category | flops | bytes accessed | tf_op | source)
XLA Modules:
  0.0 52.8 jit_solution(915692949677142166)
XLA Ops:
  0.0 0.0 copy-start
  0.0 0.0 copy-start.2
  0.0 7.6 %all_gather.6.gathered_ref = f32[4,8,16,256]{3,2,1,0:T(8,128)S(1)} all-gather(f32[1,8,16,256]{3,2,1,0:T(8,128)} %param.7), channel_id=1, replica_groups={{0,32,64,96},{128,160,192,224},{256,288,320,352},{384,416,448,480},{512..., dimensions={0}, use_global_device_ids=true | all-gather | bytes 655360 | tf_op jit(solution)/shard_map/all_gather | solution.py:282
  7.6 0.0 copy-done
  7.6 0.0 copy-done.2
  7.7 0.0 copy-start.1
  7.7 0.8 %collective-permute-start = (f32[2,16,256]{2,1,0:T(8,128)S(1)}, f32[2,16,256]{2,1,0:T(8,128)S(1)}, u32[]{:S(2)}, u32[]{:S(2)}) collective-permute-start(f32[2,16,256]{2,1,0:T(8,128)S(1)} %get-tuple-element.24), channel_id=1, source_target_pairs={{0,128},{32,160},{64,192},{96,224},{1,129},{33,161},{65,193},{97,2... | collective-permute-start | bytes 98312 | tf_op jit(solution)/shard_map/ppermute | solution.py:298
  8.5 0.0 collective-permute-done
  8.5 0.7 %collective-permute-start.1 = (f32[2,16,256]{2,1,0:T(8,128)S(1)}, f32[2,16,256]{2,1,0:T(8,128)S(1)}, u32[]{:S(2)}, u32[]{:S(2)}) collective-permute-start(f32[2,16,256]{2,1,0:T(8,128)S(1)} %get-tuple-element.22), channel_id=1, source_target_pairs={{128,256},{160,288},{192,320},{224,352},{129,257},{161,289},{193,3... | collective-permute-start | bytes 98312 | tf_op jit(solution)/shard_map/ppermute | solution.py:298
  9.2 0.0 copy-done.1
  9.2 3.5 %collective-permute-start.6 = (f32[8,16,256]{2,1,0:T(8,128)S(1)}, f32[8,16,256]{2,1,0:T(8,128)S(1)}, u32[]{:S(2)}, u32[]{:S(2)}) collective-permute-start(f32[8,16,256]{2,1,0:T(8,128)S(1)} %bitcast.37), channel_id=1, source_target_pairs={{96,128},{224,256},{352,384},{480,512},{608,640},{736,768},{864,89... | collective-permute-start | bytes 393224 | tf_op jit(solution)/shard_map/ppermute | solution.py:281
  12.8 0.0 collective-permute-done.1
  12.8 0.7 %collective-permute-start.2 = (f32[2,16,256]{2,1,0:T(8,128)S(1)}, f32[2,16,256]{2,1,0:T(8,128)S(1)}, u32[]{:S(2)}, u32[]{:S(2)}) collective-permute-start(f32[2,16,256]{2,1,0:T(8,128)S(1)} %multiply_add_fusion.2), channel_id=1, source_target_pairs={{256,384},{288,416},{320,448},{352,480},{257,385},{289,417},{321,4... | collective-permute-start | bytes 98312 | tf_op jit(solution)/shard_map/ppermute | solution.py:298
  13.5 1.3 %collective-permute-start.4 = (f32[2,16,256]{2,1,0:T(8,128)S(1)}, f32[2,16,256]{2,1,0:T(8,128)S(1)}, u32[]{:S(2)}, u32[]{:S(2)}) collective-permute-start(f32[2,16,256]{2,1,0:T(8,128)S(1)} %get-tuple-element.25), channel_id=1, source_target_pairs={{512,640},{544,672},{576,704},{608,736},{768,896},{800,928},{832,9... | collective-permute-start | bytes 98312 | tf_op jit(solution)/shard_map/ppermute | solution.py:298
  14.8 0.0 collective-permute-done.2
  14.8 0.0 collective-permute-done.6.handover_ref
  14.8 0.7 %collective-permute-start.3 = (f32[2,16,256]{2,1,0:T(8,128)S(1)}, f32[2,16,256]{2,1,0:T(8,128)S(1)}, u32[]{:S(2)}, u32[]{:S(2)}) collective-permute-start(f32[2,16,256]{2,1,0:T(8,128)S(1)} %get-tuple-element.20), channel_id=1, source_target_pairs={{384,640},{416,672},{448,704},{480,736},{385,641},{417,673},{449,7... | collective-permute-start | bytes 98312 | tf_op jit(solution)/shard_map/ppermute | solution.py:298
  15.5 0.7 %collective-permute-start.7 = (f32[2,16,256]{2,1,0:T(8,128)S(1)}, f32[2,16,256]{2,1,0:T(8,128)S(1)}, u32[]{:S(2)}, u32[]{:S(2)}) collective-permute-start(f32[2,16,256]{2,1,0:T(8,128)S(1)} %get-tuple-element.19), channel_id=1, source_target_pairs={{384,512},{416,544},{448,576},{480,608},{385,513},{417,545},{449,5... | collective-permute-start | bytes 98312 | tf_op jit(solution)/shard_map/ppermute | solution.py:298
  16.2 0.0 collective-permute-done.4
  16.2 0.0 collective-permute-done.3
  16.2 0.7 %collective-permute-start.8 = (f32[2,16,256]{2,1,0:T(8,128)S(1)}, f32[2,16,256]{2,1,0:T(8,128)S(1)}, u32[]{:S(2)}, u32[]{:S(2)}) collective-permute-start(f32[2,16,256]{2,1,0:T(8,128)S(1)} %multiply_add_fusion), channel_id=1, source_target_pairs={{640,896},{672,928},{704,960},{736,992},{641,897},{673,929},{705,9... | collective-permute-start | bytes 98312 | tf_op jit(solution)/shard_map/ppermute | solution.py:298
  16.9 1.3 %collective-permute-start.5 = (f32[2,16,256]{2,1,0:T(8,128)S(1)}, f32[2,16,256]{2,1,0:T(8,128)S(1)}, u32[]{:S(2)}, u32[]{:S(2)}) collective-permute-start(f32[2,16,256]{2,1,0:T(8,128)S(1)} %multiply_add_fusion), channel_id=1, source_target_pairs={{640,768},{672,800},{704,832},{736,864},{641,769},{673,801},{705,8... | collective-permute-start | bytes 98312 | tf_op jit(solution)/shard_map/ppermute | solution.py:298
  18.2 0.1 stack.19.place_ref
  18.3 0.0 collective-permute-done.7
  18.3 0.0 collective-permute-done.8
  18.3 10.5 %collective-permute-done.5 = f32[2,16,256]{2,1,0:T(8,128)S(1)} collective-permute-done((f32[2,16,256]{2,1,0:T(8,128)S(1)}, f32[2,16,256]{2,1,0:T(8,128)S(1)}, u32[]{:S(2)}, u32[]{:S(2)}) %collective-permute-start.5) | collective-permute-done | bytes 32800 | tf_op jit(solution)/shard_map/ppermute | solution.py:298
  28.8 0.0 copy-start.3
  28.8 0.0 copy-start.4
  28.8 0.0 copy-start.5
  28.9 7.3 %all_gather.7.base_ref = f32[8,16,256]{2,1,0:T(8,128)S(1)} all-gather(f32[2,16,256]{2,1,0:T(8,128)S(1)} %select_select_fusion), channel_id=1, replica_groups={{0,32,64,96},{128,160,192,224},{256,288,320,352},{384,416,448,480},{512..., dimensions={0}, use_global_device_ids=true | all-gather | bytes 163840 | tf_op jit(solution)/shard_map/all_gather | solution.py:317
  36.1 0.0 copy-done.3
  36.1 0.0 copy-done.4
  36.1 0.0 copy-done.5
  36.1 0.7 %shard_map.64 = (f32[8,16,256]{2,1,0:T(8,128)S(1)}, f32[8,16,256]{2,1,0:T(8,128)S(1)}, f32[8,16,256]{2,1,0:T(8,128)S(1)}, f32[4,8,2,256]{3,2,1,0:T(2,128)S(1)}, f32[4,8,2,256]{3,2,1,0:T(2,128)S(1)}) custom-call(s32[5]{0:T(128)S(1)} %stack.19.place_ref, f32[8,16,256]{2,1,0:T(8,128)S(1)} %all_gather.7.base_ref, f32[4,8,16,256]{3,2,1,0:T(8,128)S(1)} %all_gather.6.gathered_ref, ...), custom_call_target="tpu_custom_call" | custom-call | flops 1048576 | bytes 131072 | tf_op jit(solution)/shard_map/pallas_call | solution.py:334
  36.8 3.1 %collective-permute-start.9 = (f32[4,8,2,256]{3,2,1,0:T(2,128)S(1)}, f32[4,8,2,256]{3,2,1,0:T(2,128)S(1)}, u32[]{:S(2)}, u32[]{:S(2)}) collective-permute-start(f32[4,8,2,256]{3,2,1,0:T(2,128)S(1)} %get-tuple-element.15), channel_id=1, source_target_pairs={{0,8},{8,16},{16,24},{1,9},{9,17},{17,25},{2,10},{10,18},{18,26},{... | collective-permute-start | bytes 196616 | tf_op jit(solution)/shard_map/ppermute | solution.py:339
  40.0 4.7 %collective-permute-start.10 = (f32[4,8,2,256]{3,2,1,0:T(2,128)S(1)}, f32[4,8,2,256]{3,2,1,0:T(2,128)S(1)}, u32[]{:S(2)}, u32[]{:S(2)}) collective-permute-start(f32[4,8,2,256]{3,2,1,0:T(2,128)S(1)} %get-tuple-element.16), channel_id=1, source_target_pairs={{8,0},{16,8},{24,16},{9,1},{17,9},{25,17},{10,2},{18,10},{26,18},{... | collective-permute-start | bytes 196616 | tf_op jit(solution)/shard_map/ppermute | solution.py:340
  44.6 3.6 %shard_map.65 = (f32[8,8,16,256]{3,2,1,0:T(8,128)S(1)}, f32[8,16,256]{2,1,0:T(8,128)S(1)}) custom-call(f32[8,16,256]{2,1,0:T(8,128)S(1)} %get-tuple-element.12.start_ref, f32[8,16,256]{2,1,0:T(8,128)S(1)} %get-tuple-element.13.before_ref, f32[8,16,256]{2,1,0:T(8,128)S(1)} %bitcast.39, f32[8,16,256]{2,1,0:T(8,128)S(1)} %get-tuple-element.14.force_before_ref, ...), custom_call_target="tpu_custom_call" | custom-call | flops 33554432 | bytes 4194304 | tf_op jit(solution)/shard_map/pallas_call | solution.py:344
  48.3 0.0 collective-permute-done.9.below_ref
  48.3 0.0 collective-permute-done.10.above_ref
  48.3 4.5 %shard_map.66 = f32[1,1,8,16,256]{4,3,2,1,0:T(8,128)} custom-call(s32[5]{0:T(128)S(1)} %stack.19.place_ref, f32[8,16,256]{2,1,0:T(8,128)S(1)} %get-tuple-element.12.start_ref, f32[8,16,256]{2,1,0:T(8,128)S(1)} %get-tuple-element.13.before_ref, f32[8,16,256]{2,1,0:T(8,128)S(1)} %bitcast.40, f32[8,16,256]{2,1,0:T(8,128)S(1)} %get-tuple-element.14.force_before_ref, ...), custom_call_target="tpu_custom_call" | custom-call | flops 33554432 | bytes 4194304 | tf_op jit(solution)/shard_map/pallas_call | solution.py:349
  (6 shorter events, 0.2 us)
Async XLA Ops:
  0.0 7.6 %copy-start = (f32[8,16,256]{2,1,0:T(8,128)S(1)}, f32[8,16,256]{2,1,0:T(8,128)}, u32[]{:S(2)}) copy-start(f32[8,16,256]{2,1,0:T(8,128)} %decay_ref.5) | copy-start | bytes 393220
  0.0 7.6 %copy-start.2 = (f32[8,16,256]{2,1,0:T(8,128)S(1)}, f32[8,16,256]{2,1,0:T(8,128)}, u32[]{:S(2)}) copy-start(f32[8,16,256]{2,1,0:T(8,128)} %initial_ref.1) | copy-start | bytes 393220
  7.7 1.6 %copy-start.1 = (f32[1,8,16,256]{3,2,1,0:T(8,128)S(1)}, f32[1,8,16,256]{3,2,1,0:T(8,128)}, u32[]{:S(2)}) copy-start(f32[1,8,16,256]{3,2,1,0:T(8,128)} %param.7) | copy-start | bytes 393220
  7.7 0.8 %collective-permute-start = (f32[2,16,256]{2,1,0:T(8,128)S(1)}, f32[2,16,256]{2,1,0:T(8,128)S(1)}, u32[]{:S(2)}, u32[]{:S(2)}) collective-permute-start(f32[2,16,256]{2,1,0:T(8,128)S(1)} %get-tuple-element.24), channel_id=1, source_target_pairs={{0,128},{32,160},{64,192},{96,224},{1,129},{33,161},{65,193},{97,2... | collective-permute-start | bytes 98312 | tf_op jit(solution)/shard_map/ppermute | solution.py:298
  8.5 4.2 %collective-permute-start.1 = (f32[2,16,256]{2,1,0:T(8,128)S(1)}, f32[2,16,256]{2,1,0:T(8,128)S(1)}, u32[]{:S(2)}, u32[]{:S(2)}) collective-permute-start(f32[2,16,256]{2,1,0:T(8,128)S(1)} %get-tuple-element.22), channel_id=1, source_target_pairs={{128,256},{160,288},{192,320},{224,352},{129,257},{161,289},{193,3... | collective-permute-start | bytes 98312 | tf_op jit(solution)/shard_map/ppermute | solution.py:298
  9.2 5.6 %collective-permute-start.6 = (f32[8,16,256]{2,1,0:T(8,128)S(1)}, f32[8,16,256]{2,1,0:T(8,128)S(1)}, u32[]{:S(2)}, u32[]{:S(2)}) collective-permute-start(f32[8,16,256]{2,1,0:T(8,128)S(1)} %bitcast.37), channel_id=1, source_target_pairs={{96,128},{224,256},{352,384},{480,512},{608,640},{736,768},{864,89... | collective-permute-start | bytes 393224 | tf_op jit(solution)/shard_map/ppermute | solution.py:281
  12.8 2.0 %collective-permute-start.2 = (f32[2,16,256]{2,1,0:T(8,128)S(1)}, f32[2,16,256]{2,1,0:T(8,128)S(1)}, u32[]{:S(2)}, u32[]{:S(2)}) collective-permute-start(f32[2,16,256]{2,1,0:T(8,128)S(1)} %multiply_add_fusion.2), channel_id=1, source_target_pairs={{256,384},{288,416},{320,448},{352,480},{257,385},{289,417},{321,4... | collective-permute-start | bytes 98312 | tf_op jit(solution)/shard_map/ppermute | solution.py:298
  13.5 2.7 %collective-permute-start.4 = (f32[2,16,256]{2,1,0:T(8,128)S(1)}, f32[2,16,256]{2,1,0:T(8,128)S(1)}, u32[]{:S(2)}, u32[]{:S(2)}) collective-permute-start(f32[2,16,256]{2,1,0:T(8,128)S(1)} %get-tuple-element.25), channel_id=1, source_target_pairs={{512,640},{544,672},{576,704},{608,736},{768,896},{800,928},{832,9... | collective-permute-start | bytes 98312 | tf_op jit(solution)/shard_map/ppermute | solution.py:298
  14.8 1.4 %collective-permute-start.3 = (f32[2,16,256]{2,1,0:T(8,128)S(1)}, f32[2,16,256]{2,1,0:T(8,128)S(1)}, u32[]{:S(2)}, u32[]{:S(2)}) collective-permute-start(f32[2,16,256]{2,1,0:T(8,128)S(1)} %get-tuple-element.20), channel_id=1, source_target_pairs={{384,640},{416,672},{448,704},{480,736},{385,641},{417,673},{449,7... | collective-permute-start | bytes 98312 | tf_op jit(solution)/shard_map/ppermute | solution.py:298
  15.5 2.8 %collective-permute-start.7 = (f32[2,16,256]{2,1,0:T(8,128)S(1)}, f32[2,16,256]{2,1,0:T(8,128)S(1)}, u32[]{:S(2)}, u32[]{:S(2)}) collective-permute-start(f32[2,16,256]{2,1,0:T(8,128)S(1)} %get-tuple-element.19), channel_id=1, source_target_pairs={{384,512},{416,544},{448,576},{480,608},{385,513},{417,545},{449,5... | collective-permute-start | bytes 98312 | tf_op jit(solution)/shard_map/ppermute | solution.py:298
  16.2 2.1 %collective-permute-start.8 = (f32[2,16,256]{2,1,0:T(8,128)S(1)}, f32[2,16,256]{2,1,0:T(8,128)S(1)}, u32[]{:S(2)}, u32[]{:S(2)}) collective-permute-start(f32[2,16,256]{2,1,0:T(8,128)S(1)} %multiply_add_fusion), channel_id=1, source_target_pairs={{640,896},{672,928},{704,960},{736,992},{641,897},{673,929},{705,9... | collective-permute-start | bytes 98312 | tf_op jit(solution)/shard_map/ppermute | solution.py:298
  16.9 11.9 %collective-permute-start.5 = (f32[2,16,256]{2,1,0:T(8,128)S(1)}, f32[2,16,256]{2,1,0:T(8,128)S(1)}, u32[]{:S(2)}, u32[]{:S(2)}) collective-permute-start(f32[2,16,256]{2,1,0:T(8,128)S(1)} %multiply_add_fusion), channel_id=1, source_target_pairs={{640,768},{672,800},{704,832},{736,864},{641,769},{673,801},{705,8... | collective-permute-start | bytes 98312 | tf_op jit(solution)/shard_map/ppermute | solution.py:298
  28.8 7.3 %copy-start.3 = (f32[8,8]{1,0:T(8,128)S(1)}, f32[8,8]{1,0:T(8,128)}, u32[]{:S(2)}) copy-start(f32[8,8]{1,0:T(8,128)} %mix_hbm.5) | copy-start | bytes 772
  28.8 7.3 %copy-start.4 = (f32[3,8]{1,0:T(4,128)S(1)}, f32[3,8]{1,0:T(4,128)}, u32[]{:S(2)}) copy-start(f32[3,8]{1,0:T(4,128)} %vel_hbm.5) | copy-start | bytes 292
  28.8 7.3 %copy-start.5 = (f32[8]{0:T(128)S(1)}, f32[8]{0:T(128)}, u32[]{:S(2)}) copy-start(f32[8]{0:T(128)} %diff_hbm.5) | copy-start | bytes 100
  36.8 11.4 %collective-permute-start.9 = (f32[4,8,2,256]{3,2,1,0:T(2,128)S(1)}, f32[4,8,2,256]{3,2,1,0:T(2,128)S(1)}, u32[]{:S(2)}, u32[]{:S(2)}) collective-permute-start(f32[4,8,2,256]{3,2,1,0:T(2,128)S(1)} %get-tuple-element.15), channel_id=1, source_target_pairs={{0,8},{8,16},{16,24},{1,9},{9,17},{17,25},{2,10},{10,18},{18,26},{... | collective-permute-start | bytes 196616 | tf_op jit(solution)/shard_map/ppermute | solution.py:339
  40.0 8.3 %collective-permute-start.10 = (f32[4,8,2,256]{3,2,1,0:T(2,128)S(1)}, f32[4,8,2,256]{3,2,1,0:T(2,128)S(1)}, u32[]{:S(2)}, u32[]{:S(2)}) collective-permute-start(f32[4,8,2,256]{3,2,1,0:T(2,128)S(1)} %get-tuple-element.16), channel_id=1, source_target_pairs={{8,0},{16,8},{24,16},{9,1},{17,9},{25,17},{10,2},{18,10},{26,18},{... | collective-permute-start | bytes 196616 | tf_op jit(solution)/shard_map/ppermute | solution.py:340

commit v6 on v5

--- a/solution.py
+++ b/solution.py
@@ -108,7 +108,7 @@
         node_starts(s, points, (now, then), decay)
         return carry
 
-    lax.fori_loop(0, species, begin, 0, unroll=4)
+    lax.fori_loop(0, species, begin, 0, unroll=8)
 
     ready()
 
@@ -120,7 +120,7 @@
             v1_ref[m, s] = swept(m, weights, points, rates, start_ref[s], v_ref[m, s], decay)
         return carry
 
-    lax.fori_loop(0, species, sweep, 0, unroll=4)
+    lax.fori_loop(0, species, sweep, 0, unroll=8)
 
     def sweep_before(s, carry):
         decay = decay_ref[s]
@@ -135,7 +135,7 @@
         handed_ref[s] = (base + (moved + coupled) + stiff * w_ref[m, s]) / (1.0 + stiff)
         return carry
 
-    lax.fori_loop(0, species, sweep_before, 0, unroll=4)
+    lax.fori_loop(0, species, sweep_before, 0, unroll=8)
 
 
 def fetch(sources, targets, sems):
@@ -187,10 +187,8 @@
 
 
 def outer_kernel(place_ref, start_ref, before_ref, force_ref, force_before_ref, decay_ref,
-                 initial_ref, below_ref, above_ref, v1_ref, handed_ref, mix_hbm, diff_hbm, vel_hbm,
-                 out_ref, e_ref, v_ref, w_ref, v1e_ref, handede_ref, full_ref, mix_ref, diff_ref,
-                 vel_ref, sems):
-    ready = fetch((mix_hbm, diff_hbm, vel_hbm), (mix_ref, diff_ref, vel_ref), sems)
+                 initial_ref, below_ref, above_ref, v1_ref, handed_ref, mix_ref, diff_ref, vel_ref,
+                 out_ref, e_ref, v_ref, w_ref, v1e_ref, handede_ref, full_ref):
     node, slot, tile, tiles = place_ref[1], place_ref[2], place_ref[3], place_ref[4]
     species, planes, cells = start_ref.shape
     count = v_ref.shape[0]
@@ -206,7 +204,7 @@
             e_ref[k, s, 2:4] = ref[s, 0:2]
             e_ref[k, s, 4:6] = ref[s, planes - 2 : planes]
     first_sweep(e_ref.at[0], e_ref.at[3], e_ref.at[1], e_ref.at[4], e_ref.at[2], mix_ref, diff_ref,
-                vel_ref, v_ref, w_ref, v1e_ref, handede_ref, ready)
+                vel_ref, v_ref, w_ref, v1e_ref, handede_ref, lambda: None)
     edge = lax.broadcasted_iota(jnp.int32, (8, cells), 0)
     outside = ((tile == 0) & (edge == 1)) | ((tile == tiles - 1) & (edge == 6))
     row = lax.broadcasted_iota(jnp.int32, (planes, cells), 0)
@@ -220,7 +218,7 @@
             full_ref[j, s, planes - 1 : planes] = v1e[5:6]
         return carry
 
-    lax.fori_loop(0, species, fill, 0, unroll=4)
+    lax.fori_loop(0, species, fill, 0, unroll=8)
     weights = quadrature(count)[0]
     own_row = []
     for j in range(count):
@@ -251,7 +249,7 @@
         out_ref[0, 0, s] = (second_start + time_step * summed + stiff * own) / (1.0 + stiff)
         return carry
 
-    lax.fori_loop(0, species, finish, 0, unroll=4)
+    lax.fori_loop(0, species, finish, 0, unroll=8)
 
 
 def call(kernel, outs, ins, scratch, cost, params=()):
@@ -349,10 +347,9 @@
     (out,) = call(
         outer_kernel,
         [(1, 1) + full],
-        "s" + "v" * 10 + "hhh",
+        "s" + "v" * 10 + "sss",
         [(5,) + small, edges, edges, edges, small, nodes],
         2**25,
-        shapes,
     )(where_am_i, *fields, initial, below, above, v1, handed, *params)
     return out
 

time: 53.1 us -> 52.7 us (level)
  no operation moved by 1% of the time
where the time goes in v6:
time: 52.7 us; the launch traced here: 52.4 us
  starting transfers between devices  18 us (34%)
  blocking collectives  14.9 us (28%)
  waiting for transfers between devices  10.5 us (20%)
  Pallas kernels  8.43 us (16%)
    ppermute x8, waiting for transfers between devices, send(): return lax.ppermute(value, 'tm', pairs)  10.5 us
    all_gather x1, blocking collectives, team_base(): gathered = lax.all_gather(force, 'tm', axis_index_groups=groups)  7.62 us
    all_gather x1, blocking collectives, team_base(): lax.all_gather(state, 'tm', axis=0, tiled=True, axis_index_groups=groups)  7.29 us
    ppermute x8, starting transfers between devices, send(): return lax.ppermute(value, 'tm', pairs)  6.69 us
    ppermute x1, starting transfers between devices, body(): above = lax.ppermute(low, 'space', down)  4.66 us
    pallas_call x1, Pallas kernels, body(): call(outer_kernel, [(1, 1) + full], 's' + 'v' * 10 + 'sss', [(5,) + small...  4.11 us
    pallas_call x1, Pallas kernels, body(): call(inner_kernel, [nodes, full], 'vvvvvhhh', [nodes, nodes], 2 ** 25, sh...  3.63 us
    ppermute x1, starting transfers between devices, team_base(): lax.ppermute(force, 'tm', [(TEAM * g - 1, TEAM * g) for g in range(1, tea...  3.53 us
  transfers between devices with their start and end apart: 11, of which 1 were waited for; matrix products, arithmetic and copies ran while one was open for 0% of the time, Pallas kernels for 7%

profile of v6, /device:TPU:835, one launch (start us, length us, event | category | flops | bytes accessed | tf_op | source)
XLA Modules:
  0.0 52.4 jit_solution(6285957939346792409)
XLA Ops:
  0.0 0.0 copy-start
  0.0 0.0 copy-start.2
  0.0 7.6 %all_gather.6.gathered_ref = f32[4,8,16,256]{3,2,1,0:T(8,128)S(1)} all-gather(f32[1,8,16,256]{3,2,1,0:T(8,128)} %param.7), channel_id=1, replica_groups={{0,32,64,96},{128,160,192,224},{256,288,320,352},{384,416,448,480},{512..., dimensions={0}, use_global_device_ids=true | all-gather | bytes 655360 | tf_op jit(solution)/shard_map/all_gather | solution.py:280
  7.6 0.0 copy-done
  7.6 0.0 copy-done.2
  7.7 0.0 copy-start.1
  7.7 0.8 %collective-permute-start = (f32[2,16,256]{2,1,0:T(8,128)S(1)}, f32[2,16,256]{2,1,0:T(8,128)S(1)}, u32[]{:S(2)}, u32[]{:S(2)}) collective-permute-start(f32[2,16,256]{2,1,0:T(8,128)S(1)} %get-tuple-element.24), channel_id=1, source_target_pairs={{0,128},{32,160},{64,192},{96,224},{1,129},{33,161},{65,193},{97,2... | collective-permute-start | bytes 98312 | tf_op jit(solution)/shard_map/ppermute | solution.py:296
  8.5 0.0 collective-permute-done
  8.5 0.7 %collective-permute-start.1 = (f32[2,16,256]{2,1,0:T(8,128)S(1)}, f32[2,16,256]{2,1,0:T(8,128)S(1)}, u32[]{:S(2)}, u32[]{:S(2)}) collective-permute-start(f32[2,16,256]{2,1,0:T(8,128)S(1)} %get-tuple-element.22), channel_id=1, source_target_pairs={{128,256},{160,288},{192,320},{224,352},{129,257},{161,289},{193,3... | collective-permute-start | bytes 98312 | tf_op jit(solution)/shard_map/ppermute | solution.py:296
  9.2 0.0 copy-done.1
  9.2 3.5 %collective-permute-start.6 = (f32[8,16,256]{2,1,0:T(8,128)S(1)}, f32[8,16,256]{2,1,0:T(8,128)S(1)}, u32[]{:S(2)}, u32[]{:S(2)}) collective-permute-start(f32[8,16,256]{2,1,0:T(8,128)S(1)} %bitcast.37), channel_id=1, source_target_pairs={{96,128},{224,256},{352,384},{480,512},{608,640},{736,768},{864,89... | collective-permute-start | bytes 393224 | tf_op jit(solution)/shard_map/ppermute | solution.py:279
  12.8 0.0 collective-permute-done.1
  12.8 0.7 %collective-permute-start.2 = (f32[2,16,256]{2,1,0:T(8,128)S(1)}, f32[2,16,256]{2,1,0:T(8,128)S(1)}, u32[]{:S(2)}, u32[]{:S(2)}) collective-permute-start(f32[2,16,256]{2,1,0:T(8,128)S(1)} %multiply_add_fusion.2), channel_id=1, source_target_pairs={{256,384},{288,416},{320,448},{352,480},{257,385},{289,417},{321,4... | collective-permute-start | bytes 98312 | tf_op jit(solution)/shard_map/ppermute | solution.py:296
  13.5 1.3 %collective-permute-start.4 = (f32[2,16,256]{2,1,0:T(8,128)S(1)}, f32[2,16,256]{2,1,0:T(8,128)S(1)}, u32[]{:S(2)}, u32[]{:S(2)}) collective-permute-start(f32[2,16,256]{2,1,0:T(8,128)S(1)} %get-tuple-element.25), channel_id=1, source_target_pairs={{512,640},{544,672},{576,704},{608,736},{768,896},{800,928},{832,9... | collective-permute-start | bytes 98312 | tf_op jit(solution)/shard_map/ppermute | solution.py:296
  14.8 0.0 collective-permute-done.2
  14.8 0.0 collective-permute-done.6.handover_ref
  14.8 0.7 %collective-permute-start.3 = (f32[2,16,256]{2,1,0:T(8,128)S(1)}, f32[2,16,256]{2,1,0:T(8,128)S(1)}, u32[]{:S(2)}, u32[]{:S(2)}) collective-permute-start(f32[2,16,256]{2,1,0:T(8,128)S(1)} %get-tuple-element.20), channel_id=1, source_target_pairs={{384,640},{416,672},{448,704},{480,736},{385,641},{417,673},{449,7... | collective-permute-start | bytes 98312 | tf_op jit(solution)/shard_map/ppermute | solution.py:296
  15.5 0.7 %collective-permute-start.7 = (f32[2,16,256]{2,1,0:T(8,128)S(1)}, f32[2,16,256]{2,1,0:T(8,128)S(1)}, u32[]{:S(2)}, u32[]{:S(2)}) collective-permute-start(f32[2,16,256]{2,1,0:T(8,128)S(1)} %get-tuple-element.19), channel_id=1, source_target_pairs={{384,512},{416,544},{448,576},{480,608},{385,513},{417,545},{449,5... | collective-permute-start | bytes 98312 | tf_op jit(solution)/shard_map/ppermute | solution.py:296
  16.2 0.0 collective-permute-done.4
  16.2 0.0 collective-permute-done.3
  16.2 0.7 %collective-permute-start.8 = (f32[2,16,256]{2,1,0:T(8,128)S(1)}, f32[2,16,256]{2,1,0:T(8,128)S(1)}, u32[]{:S(2)}, u32[]{:S(2)}) collective-permute-start(f32[2,16,256]{2,1,0:T(8,128)S(1)} %multiply_add_fusion), channel_id=1, source_target_pairs={{640,896},{672,928},{704,960},{736,992},{641,897},{673,929},{705,9... | collective-permute-start | bytes 98312 | tf_op jit(solution)/shard_map/ppermute | solution.py:296
  16.9 1.3 %collective-permute-start.5 = (f32[2,16,256]{2,1,0:T(8,128)S(1)}, f32[2,16,256]{2,1,0:T(8,128)S(1)}, u32[]{:S(2)}, u32[]{:S(2)}) collective-permute-start(f32[2,16,256]{2,1,0:T(8,128)S(1)} %multiply_add_fusion), channel_id=1, source_target_pairs={{640,768},{672,800},{704,832},{736,864},{641,769},{673,801},{705,8... | collective-permute-start | bytes 98312 | tf_op jit(solution)/shard_map/ppermute | solution.py:296
  18.2 0.1 stack.19.place_ref
  18.3 0.0 collective-permute-done.7
  18.3 0.0 collective-permute-done.8
  18.3 10.5 %collective-permute-done.5 = f32[2,16,256]{2,1,0:T(8,128)S(1)} collective-permute-done((f32[2,16,256]{2,1,0:T(8,128)S(1)}, f32[2,16,256]{2,1,0:T(8,128)S(1)}, u32[]{:S(2)}, u32[]{:S(2)}) %collective-permute-start.5) | collective-permute-done | bytes 32800 | tf_op jit(solution)/shard_map/ppermute | solution.py:296
  28.8 0.0 copy-start.3
  28.8 0.0 copy-start.4
  28.8 0.0 copy-start.5
  28.9 7.3 %all_gather.7.base_ref = f32[8,16,256]{2,1,0:T(8,128)S(1)} all-gather(f32[2,16,256]{2,1,0:T(8,128)S(1)} %select_select_fusion), channel_id=1, replica_groups={{0,32,64,96},{128,160,192,224},{256,288,320,352},{384,416,448,480},{512..., dimensions={0}, use_global_device_ids=true | all-gather | bytes 163840 | tf_op jit(solution)/shard_map/all_gather | solution.py:315
  36.1 0.0 copy-done.3
  36.1 0.0 copy-done.4
  36.1 0.0 copy-done.5
  36.1 0.7 %shard_map.64 = (f32[8,16,256]{2,1,0:T(8,128)S(1)}, f32[8,16,256]{2,1,0:T(8,128)S(1)}, f32[8,16,256]{2,1,0:T(8,128)S(1)}, f32[4,8,2,256]{3,2,1,0:T(2,128)S(1)}, f32[4,8,2,256]{3,2,1,0:T(2,128)S(1)}) custom-call(s32[5]{0:T(128)S(1)} %stack.19.place_ref, f32[8,16,256]{2,1,0:T(8,128)S(1)} %all_gather.7.base_ref, f32[4,8,16,256]{3,2,1,0:T(8,128)S(1)} %all_gather.6.gathered_ref, ...), custom_call_target="tpu_custom_call" | custom-call | flops 1048576 | bytes 131072 | tf_op jit(solution)/shard_map/pallas_call | solution.py:332
  36.8 3.1 %collective-permute-start.9 = (f32[4,8,2,256]{3,2,1,0:T(2,128)S(1)}, f32[4,8,2,256]{3,2,1,0:T(2,128)S(1)}, u32[]{:S(2)}, u32[]{:S(2)}) collective-permute-start(f32[4,8,2,256]{3,2,1,0:T(2,128)S(1)} %get-tuple-element.15), channel_id=1, source_target_pairs={{0,8},{8,16},{16,24},{1,9},{9,17},{17,25},{2,10},{10,18},{18,26},{... | collective-permute-start | bytes 196616 | tf_op jit(solution)/shard_map/ppermute | solution.py:337
  40.0 4.7 %collective-permute-start.10 = (f32[4,8,2,256]{3,2,1,0:T(2,128)S(1)}, f32[4,8,2,256]{3,2,1,0:T(2,128)S(1)}, u32[]{:S(2)}, u32[]{:S(2)}) collective-permute-start(f32[4,8,2,256]{3,2,1,0:T(2,128)S(1)} %get-tuple-element.16), channel_id=1, source_target_pairs={{8,0},{16,8},{24,16},{9,1},{17,9},{25,17},{10,2},{18,10},{26,18},{... | collective-permute-start | bytes 196616 | tf_op jit(solution)/shard_map/ppermute | solution.py:338
  44.6 3.6 %shard_map.65 = (f32[8,8,16,256]{3,2,1,0:T(8,128)S(1)}, f32[8,16,256]{2,1,0:T(8,128)S(1)}) custom-call(f32[8,16,256]{2,1,0:T(8,128)S(1)} %get-tuple-element.12.start_ref, f32[8,16,256]{2,1,0:T(8,128)S(1)} %get-tuple-element.13.before_ref, f32[8,16,256]{2,1,0:T(8,128)S(1)} %bitcast.39, f32[8,16,256]{2,1,0:T(8,128)S(1)} %get-tuple-element.14.force_before_ref, ...), custom_call_target="tpu_custom_call" | custom-call | flops 33554432 | bytes 4194304 | tf_op jit(solution)/shard_map/pallas_call | solution.py:342
  48.3 0.0 collective-permute-done.9.below_ref
  48.3 0.0 collective-permute-done.10.above_ref
  48.3 4.1 %shard_map.66 = f32[1,1,8,16,256]{4,3,2,1,0:T(8,128)} custom-call(s32[5]{0:T(128)S(1)} %stack.19.place_ref, f32[8,16,256]{2,1,0:T(8,128)S(1)} %get-tuple-element.12.start_ref, f32[8,16,256]{2,1,0:T(8,128)S(1)} %get-tuple-element.13.before_ref, f32[8,16,256]{2,1,0:T(8,128)S(1)} %bitcast.40, f32[8,16,256]{2,1,0:T(8,128)S(1)} %get-tuple-element.14.force_before_ref, ...), custom_call_target="tpu_custom_call" | custom-call | flops 33554432 | bytes 4194304 | tf_op jit(solution)/shard_map/pallas_call | solution.py:347
  (6 shorter events, 0.2 us)
Async XLA Ops:
  0.0 7.6 %copy-start = (f32[8,16,256]{2,1,0:T(8,128)S(1)}, f32[8,16,256]{2,1,0:T(8,128)}, u32[]{:S(2)}) copy-start(f32[8,16,256]{2,1,0:T(8,128)} %decay_ref.5) | copy-start | bytes 393220
  0.0 7.6 %copy-start.2 = (f32[8,16,256]{2,1,0:T(8,128)S(1)}, f32[8,16,256]{2,1,0:T(8,128)}, u32[]{:S(2)}) copy-start(f32[8,16,256]{2,1,0:T(8,128)} %initial_ref.1) | copy-start | bytes 393220
  7.7 1.6 %copy-start.1 = (f32[1,8,16,256]{3,2,1,0:T(8,128)S(1)}, f32[1,8,16,256]{3,2,1,0:T(8,128)}, u32[]{:S(2)}) copy-start(f32[1,8,16,256]{3,2,1,0:T(8,128)} %param.7) | copy-start | bytes 393220
  7.7 0.8 %collective-permute-start = (f32[2,16,256]{2,1,0:T(8,128)S(1)}, f32[2,16,256]{2,1,0:T(8,128)S(1)}, u32[]{:S(2)}, u32[]{:S(2)}) collective-permute-start(f32[2,16,256]{2,1,0:T(8,128)S(1)} %get-tuple-element.24), channel_id=1, source_target_pairs={{0,128},{32,160},{64,192},{96,224},{1,129},{33,161},{65,193},{97,2... | collective-permute-start | bytes 98312 | tf_op jit(solution)/shard_map/ppermute | solution.py:296
  8.5 4.2 %collective-permute-start.1 = (f32[2,16,256]{2,1,0:T(8,128)S(1)}, f32[2,16,256]{2,1,0:T(8,128)S(1)}, u32[]{:S(2)}, u32[]{:S(2)}) collective-permute-start(f32[2,16,256]{2,1,0:T(8,128)S(1)} %get-tuple-element.22), channel_id=1, source_target_pairs={{128,256},{160,288},{192,320},{224,352},{129,257},{161,289},{193,3... | collective-permute-start | bytes 98312 | tf_op jit(solution)/shard_map/ppermute | solution.py:296
  9.2 5.6 %collective-permute-start.6 = (f32[8,16,256]{2,1,0:T(8,128)S(1)}, f32[8,16,256]{2,1,0:T(8,128)S(1)}, u32[]{:S(2)}, u32[]{:S(2)}) collective-permute-start(f32[8,16,256]{2,1,0:T(8,128)S(1)} %bitcast.37), channel_id=1, source_target_pairs={{96,128},{224,256},{352,384},{480,512},{608,640},{736,768},{864,89... | collective-permute-start | bytes 393224 | tf_op jit(solution)/shard_map/ppermute | solution.py:279
  12.8 2.0 %collective-permute-start.2 = (f32[2,16,256]{2,1,0:T(8,128)S(1)}, f32[2,16,256]{2,1,0:T(8,128)S(1)}, u32[]{:S(2)}, u32[]{:S(2)}) collective-permute-start(f32[2,16,256]{2,1,0:T(8,128)S(1)} %multiply_add_fusion.2), channel_id=1, source_target_pairs={{256,384},{288,416},{320,448},{352,480},{257,385},{289,417},{321,4... | collective-permute-start | bytes 98312 | tf_op jit(solution)/shard_map/ppermute | solution.py:296
  13.5 2.7 %collective-permute-start.4 = (f32[2,16,256]{2,1,0:T(8,128)S(1)}, f32[2,16,256]{2,1,0:T(8,128)S(1)}, u32[]{:S(2)}, u32[]{:S(2)}) collective-permute-start(f32[2,16,256]{2,1,0:T(8,128)S(1)} %get-tuple-element.25), channel_id=1, source_target_pairs={{512,640},{544,672},{576,704},{608,736},{768,896},{800,928},{832,9... | collective-permute-start | bytes 98312 | tf_op jit(solution)/shard_map/ppermute | solution.py:296
  14.8 1.4 %collective-permute-start.3 = (f32[2,16,256]{2,1,0:T(8,128)S(1)}, f32[2,16,256]{2,1,0:T(8,128)S(1)}, u32[]{:S(2)}, u32[]{:S(2)}) collective-permute-start(f32[2,16,256]{2,1,0:T(8,128)S(1)} %get-tuple-element.20), channel_id=1, source_target_pairs={{384,640},{416,672},{448,704},{480,736},{385,641},{417,673},{449,7... | collective-permute-start | bytes 98312 | tf_op jit(solution)/shard_map/ppermute | solution.py:296
  15.5 2.8 %collective-permute-start.7 = (f32[2,16,256]{2,1,0:T(8,128)S(1)}, f32[2,16,256]{2,1,0:T(8,128)S(1)}, u32[]{:S(2)}, u32[]{:S(2)}) collective-permute-start(f32[2,16,256]{2,1,0:T(8,128)S(1)} %get-tuple-element.19), channel_id=1, source_target_pairs={{384,512},{416,544},{448,576},{480,608},{385,513},{417,545},{449,5... | collective-permute-start | bytes 98312 | tf_op jit(solution)/shard_map/ppermute | solution.py:296
  16.2 2.1 %collective-permute-start.8 = (f32[2,16,256]{2,1,0:T(8,128)S(1)}, f32[2,16,256]{2,1,0:T(8,128)S(1)}, u32[]{:S(2)}, u32[]{:S(2)}) collective-permute-start(f32[2,16,256]{2,1,0:T(8,128)S(1)} %multiply_add_fusion), channel_id=1, source_target_pairs={{640,896},{672,928},{704,960},{736,992},{641,897},{673,929},{705,9... | collective-permute-start | bytes 98312 | tf_op jit(solution)/shard_map/ppermute | solution.py:296
  16.9 11.9 %collective-permute-start.5 = (f32[2,16,256]{2,1,0:T(8,128)S(1)}, f32[2,16,256]{2,1,0:T(8,128)S(1)}, u32[]{:S(2)}, u32[]{:S(2)}) collective-permute-start(f32[2,16,256]{2,1,0:T(8,128)S(1)} %multiply_add_fusion), channel_id=1, source_target_pairs={{640,768},{672,800},{704,832},{736,864},{641,769},{673,801},{705,8... | collective-permute-start | bytes 98312 | tf_op jit(solution)/shard_map/ppermute | solution.py:296
  28.8 7.3 %copy-start.3 = (f32[8,8]{1,0:T(8,128)S(1)}, f32[8,8]{1,0:T(8,128)}, u32[]{:S(2)}) copy-start(f32[8,8]{1,0:T(8,128)} %mix_ref.1) | copy-start | bytes 772
  28.8 7.3 %copy-start.4 = (f32[3,8]{1,0:T(4,128)S(1)}, f32[3,8]{1,0:T(4,128)}, u32[]{:S(2)}) copy-start(f32[3,8]{1,0:T(4,128)} %vel_ref.1) | copy-start | bytes 292
  28.8 7.3 %copy-start.5 = (f32[8]{0:T(128)S(1)}, f32[8]{0:T(128)}, u32[]{:S(2)}) copy-start(f32[8]{0:T(128)} %diff_ref.1) | copy-start | bytes 100
  36.8 11.4 %collective-permute-start.9 = (f32[4,8,2,256]{3,2,1,0:T(2,128)S(1)}, f32[4,8,2,256]{3,2,1,0:T(2,128)S(1)}, u32[]{:S(2)}, u32[]{:S(2)}) collective-permute-start(f32[4,8,2,256]{3,2,1,0:T(2,128)S(1)} %get-tuple-element.15), channel_id=1, source_target_pairs={{0,8},{8,16},{16,24},{1,9},{9,17},{17,25},{2,10},{10,18},{18,26},{... | collective-permute-start | bytes 196616 | tf_op jit(solution)/shard_map/ppermute | solution.py:337
  40.0 8.3 %collective-permute-start.10 = (f32[4,8,2,256]{3,2,1,0:T(2,128)S(1)}, f32[4,8,2,256]{3,2,1,0:T(2,128)S(1)}, u32[]{:S(2)}, u32[]{:S(2)}) collective-permute-start(f32[4,8,2,256]{3,2,1,0:T(2,128)S(1)} %get-tuple-element.16), channel_id=1, source_target_pairs={{8,0},{16,8},{24,16},{9,1},{17,9},{25,17},{10,2},{18,10},{26,18},{... | collective-permute-start | bytes 196616 | tf_op jit(solution)/shard_map/ppermute | solution.py:338
